TPU v7x, 512 devices: a whole 4x4x16 slice. The times are simulated.
512 devices in a mesh: space: 64 (over z, x_hi, core), scen: 8 (over x_lo, y).
Axes of the slice: x: 4 (x_hi: 2, x_lo: 2; x = x_hi * 2 + x_lo), y: 4, z: 16, core: 2. Of those that a mesh axis runs over, the one named last changes fastest.
Arguments:
- dwell_map: bfloat16 [16384, 1024], P('space', 'scen'), may hold values from 0 to 1
- target_map: bfloat16 [16384, 1024], P('space'), may hold values from -6 to 6
- bound_mask: int32 [16384, 1024], P('space', 'scen'), may hold values 0 or 1
- offsets: int32 [16, 2], replicated, may hold values from -32 to 32, as said below
- rate_index: int32 [16, 1], replicated, may hold values from 0 to 3
- rate_table: float32 [4], replicated, may hold values from 0.5 to 2
- row_kernels: bfloat16 [4, 63], replicated, may hold values from -0.75 to 0.75
- col_kernels: bfloat16 [4, 63], replicated, may hold values from -0.75 to 0.75
Outputs:
- dwell_next: bfloat16 [16384, 1024], P('space', 'scen')
Inputs may be any that keep to these rules, and one draw needn't show every extreme that they name: `offsets`: each entry lies between -32 and 32; in each column some scenario has 32 and another -32. `rate_index`: every level is used by some scenario.
All inputs are finite; a program needn't handle non-finite values. No bound on the sum of `bound_mask` on one device may be relied on, other than what follows from the above.
Results may differ from a plain program's by a relative error of at most 0.014.
Values may be sent and summed in bfloat16 or wider, within the bound.
A program may use at most 64 MiB of HBM per device.

v0:
```python
import jax
import jax.numpy as jnp
from jax import lax
from jax.sharding import PartitionSpec as P

S_DEV = 2
KTAPS = 63
REACH = 32


step_size = 1.0


def extended(x, sides, width):
    for axis, dim in sides:
        count, length = (lax.axis_size(axis), x.shape[dim])
        up = [(i, (i + 1) % count) for i in range(count - 1)]
        down = [(j, i) for i, j in up]
        last = lax.slice_in_dim(x, length - width, length, axis=dim)
        first = lax.slice_in_dim(x, 0, width, axis=dim)
        before = lax.ppermute(last, axis, up)
        after = lax.ppermute(first, axis, down)
        x = jnp.concatenate([before, x, after], axis=dim)
    return x


def band_line(kernel, start_at, row_count, col_count):
    kernel_line = jnp.zeros((col_count + 1,), kernel.dtype)
    kernel_line = lax.dynamic_update_slice(kernel_line, kernel, (start_at,))
    return jnp.tile(kernel_line, row_count)[: row_count * col_count].reshape(row_count, col_count)


def column_pass(values, kernels, shifts):
    scen_count, height, col_total = values.shape
    col_block = 128
    padded = jnp.pad(values, ((0, 0), (0, 0), (col_block, col_block)))

    def column_one_band(kernel, shift):
        return band_line(kernel, shift + col_block, col_block, 3 * col_block)

    matrices = jax.vmap(column_one_band)(kernels, shifts)
    product = jnp.zeros((scen_count, height, col_total // col_block, col_block), jnp.float32)
    for piece in range(3):
        view = padded[:, :, piece * col_block : piece * col_block + col_total].reshape(
            scen_count, height, col_total // col_block, col_block
        )
        part_mat = matrices[:, :, piece * col_block : (piece + 1) * col_block]
        product = product + jnp.einsum(
            "srny,scy->srnc", view, part_mat, preferred_element_type=jnp.float32
        )
    return product.reshape(scen_count, height, col_total)


def row_pass(values, kernels, shifts, out_rows):
    in_rows = values.shape[-2]
    rim_depth = (in_rows - out_rows) // 2
    row_block = 128
    block_count = -(-out_rows // row_block)
    window = row_block + 2 * rim_depth
    if values.ndim == 2:
        padded = values
    else:
        padded = values

    def row_one_band(kernel, shift):
        return band_line(kernel, shift + rim_depth, row_block, window)

    matrices = jax.vmap(row_one_band)(kernels, shifts)
    results = []
    for block_id in range(block_count):
        begin = block_id * row_block
        if values.ndim == 2:
            view = padded[begin : begin + window]
            results.append(
                jnp.einsum("sie,ew->siw", matrices, view, preferred_element_type=jnp.float32)
            )
        else:
            view = padded[:, begin : begin + window]
            results.append(
                jnp.einsum("sie,sew->siw", matrices, view, preferred_element_type=jnp.float32)
            )
    return jnp.concatenate(results, axis=1)


def shards(
    dwell_map, target_map, bound_mask, offsets, rate_index, rate_table, row_kernels, col_kernels
):
    tile_rows = dwell_map.shape[0]
    radius = (KTAPS - 1) // 2
    halo_rows = REACH + radius
    scen_count = S_DEV * lax.axis_size("scen")
    first_scen = lax.axis_index("scen") * S_DEV
    my_offsets = lax.dynamic_slice_in_dim(offsets, first_scen, S_DEV, 0)
    shift_rows = my_offsets[:, 0]
    shift_cols = my_offsets[:, 1]
    level_ids = lax.dynamic_slice_in_dim(rate_index, first_scen, S_DEV, 0)[:, 0]
    onehot = (
        level_ids[:, None] == jnp.arange(rate_table.shape[0], dtype=jnp.int32)[None, :]
    ).astype(jnp.float32)
    my_rates = jnp.sum(onehot * rate_table[None, :], axis=1)
    my_row_taps = jnp.sum(
        onehot[:, :, None] * row_kernels.astype(jnp.float32)[None], axis=1
    ).astype(jnp.bfloat16)
    my_col_taps = jnp.sum(
        onehot[:, :, None] * col_kernels.astype(jnp.float32)[None], axis=1
    ).astype(jnp.bfloat16)
    full_map = lax.all_gather(dwell_map, "scen", axis=1, tiled=True)
    rim_rows = extended(full_map, (("space", 0),), halo_rows)
    forward = row_pass(rim_rows, my_row_taps, -radius - shift_rows, tile_rows).astype(jnp.bfloat16)
    removal = my_rates[:, None, None] * column_pass(forward, my_col_taps, -radius - shift_cols)
    misfit = (removal - target_map.astype(jnp.float32)[None]).astype(jnp.bfloat16)
    misfit_rows = extended(misfit, (("space", 1),), halo_rows)
    back_cols = column_pass(misfit_rows, my_col_taps[:, ::-1], -radius + shift_cols).astype(
        jnp.bfloat16
    )
    adjoint = row_pass(back_cols, my_row_taps[:, ::-1], -radius + shift_rows, tile_rows)
    group_sum = jnp.sum((my_rates / scen_count)[:, None, None] * adjoint, axis=0)
    gradient = lax.psum_scatter(
        group_sum.astype(jnp.bfloat16), "scen", scatter_dimension=1, tiled=True
    ).astype(jnp.float32)
    stepped = dwell_map.astype(jnp.float32) - step_size * gradient
    return jnp.where(bound_mask == 1, jnp.maximum(stepped, 0.0), stepped).astype(jnp.bfloat16)


def solution(mesh):
    return jax.shard_map(
        shards,
        mesh=mesh,
        in_specs=(
            P("space", "scen"),
            P("space", None),
            P("space", "scen"),
            P(),
            P(),
            P(),
            P(),
            P(),
        ),
        out_specs=P("space", "scen"),
        check_vma=False,
    )
```

profile of v0, /device:TPU:32, one launch (start us, length us, event | category | flops | bytes accessed | tf_op | source)
XLA Modules:
  0.0 196.9 jit_solution(3160482951217890527)
XLA Ops:
  6.5 26.4 %all_gather.3 = bf16[256,1024]{1,0:T(8,128)(2,1)S(1)} all-gather(bf16[256,128]{1,0:T(8,128)(2,1)} %param.8), channel_id=1, replica_groups=mesh['space'=64,'scen'=8] {'scen'}, dimensions={1}, use_global_device_ids=true | all-gather | bytes 589824 | tf_op jit(solution)/shard_map/all_gather | solution.py:107
  33.0 1.9 collective-permute-start
  34.9 6.0 %collective-permute-start.1 = (bf16[63,1024]{1,0:T(8,128)(2,1)S(1)}, bf16[63,1024]{1,0:T(8,128)(2,1)S(1)}, u32[]{:S(2)}, u32[]{:S(2)}) collective-permute-start(bf16[63,1024]{1,0:T(8,128)(2,1)S(1)} %get-tuple-element.86), channel_id=1, source_target_pairs={{8,0},{16,8},{24,16},{32,24},{40,32},{48,40},{56,48},{64,56},{72,6... | collective-permute-start | bytes 387080 | tf_op jit(solution)/shard_map/ppermute | solution.py:22
  43.6 13.6 %while.5 = (s32[]{:T(128)}, bf16[2,255]{1,0:T(2,128)(2,1)S(1)}, s32[2,2]{1,0:T(2,128)S(1)}, bf16[2,63]{1,0:T(2,128)(2,1)S(1)}, s32[]{:T(128)}, /*index=5*/s32[2]{0:T(128)}) while((s32[]{:T(128)}, bf16[2,255]{1,0:T(2,128)(2,1)S(1)}, s32[2,2]{1,0:T(2,128)S(1)}, bf16[2,63]{1,0:T(2,128)(2,1)S(1)}, s32[]{:T(128)}, /*index=5*/s32[2]{0:T(128)}) %tuple.77), condition=%wide.while_cond.1, body=%wide.while_body.1.sunk | while | flops 74 | bytes 769 | solution.py:29
  44.2 2.7 %and_reduce_fusion.9 = pred[]{:T(512)} fusion(s32[2]{0:T(128)} %get-tuple-element.250, s32[1]{0:T(128)} %bitcast.121, s32[1]{0:T(128)} %bitcast.122), kind=kLoop, calls=%fused_computation.3.clone.1 | loop fusion | flops 9 | bytes 17 | tf_op jit(solution)/shard_map/vmap(vmap())/scatter
  46.9 2.0 broadcast_select_fusion.9
  51.0 2.7 %and_reduce_fusion.9 = pred[]{:T(512)} fusion(s32[2]{0:T(128)} %get-tuple-element.250, s32[1]{0:T(128)} %bitcast.121, s32[1]{0:T(128)} %bitcast.122), kind=kLoop, calls=%fused_computation.3.clone.1 | loop fusion | flops 9 | bytes 17 | tf_op jit(solution)/shard_map/vmap(vmap())/scatter
  53.7 2.0 broadcast_select_fusion.9
  57.3 13.7 %while.6 = (s32[]{:T(128)}, bf16[2,385]{1,0:T(2,128)(2,1)S(1)}, s32[2,2]{1,0:T(2,128)S(1)}, bf16[2,63]{1,0:T(2,128)(2,1)S(1)}, s32[]{:T(128)}, /*index=5*/s32[2]{0:T(128)}) while((s32[]{:T(128)}, bf16[2,385]{1,0:T(2,128)(2,1)S(1)}, s32[2,2]{1,0:T(2,128)S(1)}, bf16[2,63]{1,0:T(2,128)(2,1)S(1)}, s32[]{:T(128)}, /*index=5*/s32[2]{0:T(128)}) %tuple.80), condition=%wide.while_cond.2, body=%wide.while_body.2.sunk | while | flops 74 | bytes 769 | solution.py:29
  57.9 2.7 %and_reduce_fusion.10 = pred[]{:T(512)} fusion(s32[2]{0:T(128)} %get-tuple-element.268, s32[1]{0:T(128)} %bitcast.125, s32[1]{0:T(128)} %bitcast.126), kind=kLoop, calls=%fused_computation.6.clone.1 | loop fusion | flops 9 | bytes 17 | tf_op jit(solution)/shard_map/vmap(vmap())/scatter
  60.6 2.0 %broadcast_select_fusion.10 = bf16[1,63]{1,0:T(2,128)(2,1)S(1)} fusion(pred[]{:T(512)} %and_reduce_fusion.10, bf16[2,63]{1,0:T(2,128)(2,1)S(1)} %get-tuple-element.266, s32[]{:T(128)} %get-tuple-element.257, bf16[2,385]{1,0:T(2,128)(2,1)S(1)} %get-tuple-element.258, s32[]{:T(128)} %bitcast.127, s32[]{:T(128)} %bitcast.128), kind=kLoop, calls=%fused_computation.7.clone.1 | loop fusion | flops 63 | bytes 391 | tf_op jit(solution)/shard_map/vmap(vmap())/scatter
  64.8 2.7 %and_reduce_fusion.10 = pred[]{:T(512)} fusion(s32[2]{0:T(128)} %get-tuple-element.268, s32[1]{0:T(128)} %bitcast.125, s32[1]{0:T(128)} %bitcast.126), kind=kLoop, calls=%fused_computation.6.clone.1 | loop fusion | flops 9 | bytes 17 | tf_op jit(solution)/shard_map/vmap(vmap())/scatter
  67.5 2.0 %broadcast_select_fusion.10 = bf16[1,63]{1,0:T(2,128)(2,1)S(1)} fusion(pred[]{:T(512)} %and_reduce_fusion.10, bf16[2,63]{1,0:T(2,128)(2,1)S(1)} %get-tuple-element.266, s32[]{:T(128)} %get-tuple-element.257, bf16[2,385]{1,0:T(2,128)(2,1)S(1)} %get-tuple-element.258, s32[]{:T(128)} %bitcast.127, s32[]{:T(128)} %bitcast.128), kind=kLoop, calls=%fused_computation.7.clone.1 | loop fusion | flops 63 | bytes 391 | tf_op jit(solution)/shard_map/vmap(vmap())/scatter
  71.1 13.5 %while.7 = (s32[]{:T(128)}, bf16[2,385]{1,0:T(2,128)(2,1)S(1)}, s32[2,2]{1,0:T(2,128)S(1)}, bf16[2,63]{1,0:T(2,128)(2,1)S(1)}, s32[]{:T(128)}, /*index=5*/s32[2]{0:T(128)}) while((s32[]{:T(128)}, bf16[2,385]{1,0:T(2,128)(2,1)S(1)}, s32[2,2]{1,0:T(2,128)S(1)}, bf16[2,63]{1,0:T(2,128)(2,1)S(1)}, s32[]{:T(128)}, /*index=5*/s32[2]{0:T(128)}) %tuple.89), condition=%wide.while_cond.3, body=%wide.while_body.3.sunk | while | flops 74 | bytes 769 | solution.py:29
  71.7 2.6 %and_reduce_fusion.11 = pred[]{:T(512)} fusion(s32[2]{0:T(128)} %get-tuple-element.286, s32[1]{0:T(128)} %bitcast.129, s32[1]{0:T(128)} %bitcast.130), kind=kLoop, calls=%fused_computation.9.clone.1 | loop fusion | flops 9 | bytes 17 | tf_op jit(solution)/shard_map/vmap(vmap())/scatter
  74.4 1.9 broadcast_select_fusion.11
  78.5 2.6 %and_reduce_fusion.11 = pred[]{:T(512)} fusion(s32[2]{0:T(128)} %get-tuple-element.286, s32[1]{0:T(128)} %bitcast.129, s32[1]{0:T(128)} %bitcast.130), kind=kLoop, calls=%fused_computation.9.clone.1 | loop fusion | flops 9 | bytes 17 | tf_op jit(solution)/shard_map/vmap(vmap())/scatter
  91.3 1.9 collective-permute-start.2
  93.2 6.2 %collective-permute-start.3 = (bf16[2,63,1024]{1,2,0:T(8,128)(2,1)S(1)}, bf16[2,63,1024]{1,2,0:T(8,128)(2,1)}, u32[]{:S(2)}, u32[]{:S(2)}) collective-permute-start(bf16[2,63,1024]{1,2,0:T(8,128)(2,1)S(1)} %get-tuple-element.84), channel_id=1, source_target_pairs={{8,0},{16,8},{24,16},{32,24},{40,32},{48,40},{56,48},{64,56},{72,6... | collective-permute-start | bytes 774152 | tf_op jit(solution)/shard_map/ppermute | solution.py:22
  99.4 12.5 %while.4 = (s32[]{:T(128)}, bf16[2,255]{1,0:T(2,128)(2,1)S(1)}, s32[2,2]{1,0:T(2,128)S(1)}, bf16[2,63]{1,0:T(2,128)(2,1)S(1)}, s32[]{:T(128)}, /*index=5*/s32[2]{0:T(128)S(1)}) while((s32[]{:T(128)}, bf16[2,255]{1,0:T(2,128)(2,1)S(1)}, s32[2,2]{1,0:T(2,128)S(1)}, bf16[2,63]{1,0:T(2,128)(2,1)S(1)}, s32[]{:T(128)}, /*index=5*/s32[2]{0:T(128)S(1)}) %tuple.88), condition=%wide.while_cond, body=%wide.while_body.sunk | while | flops 74 | bytes 769 | solution.py:29
  100.1 2.0 %and_reduce_fusion.8 = pred[]{:T(512)} fusion(s32[2]{0:T(128)S(1)} %get-tuple-element.232, s32[1]{0:T(128)} %bitcast.117, s32[1]{0:T(128)} %bitcast.118), kind=kLoop, calls=%fused_computation.clone.1 | loop fusion | flops 9 | bytes 17 | tf_op jit(solution)/shard_map/vmap(vmap())/scatter
  102.1 2.0 %broadcast_select_fusion.8 = bf16[1,63]{1,0:T(2,128)(2,1)S(1)} fusion(pred[]{:T(512)} %and_reduce_fusion.8, bf16[2,63]{1,0:T(2,128)(2,1)S(1)} %get-tuple-element.230, s32[]{:T(128)} %get-tuple-element.221, bf16[2,255]{1,0:T(2,128)(2,1)S(1)} %get-tuple-element.222, s32[]{:T(128)} %bitcast.119, s32[]{:T(128)} %bitcast.120), kind=kLoop, calls=%fused_computation.1.clone.1 | loop fusion | flops 63 | bytes 391 | tf_op jit(solution)/shard_map/vmap(vmap())/scatter
  106.4 2.0 %and_reduce_fusion.8 = pred[]{:T(512)} fusion(s32[2]{0:T(128)S(1)} %get-tuple-element.232, s32[1]{0:T(128)} %bitcast.117, s32[1]{0:T(128)} %bitcast.118), kind=kLoop, calls=%fused_computation.clone.1 | loop fusion | flops 9 | bytes 17 | tf_op jit(solution)/shard_map/vmap(vmap())/scatter
  108.5 2.0 %broadcast_select_fusion.8 = bf16[1,63]{1,0:T(2,128)(2,1)S(1)} fusion(pred[]{:T(512)} %and_reduce_fusion.8, bf16[2,63]{1,0:T(2,128)(2,1)S(1)} %get-tuple-element.230, s32[]{:T(128)} %get-tuple-element.221, bf16[2,255]{1,0:T(2,128)(2,1)S(1)} %get-tuple-element.222, s32[]{:T(128)} %bitcast.119, s32[]{:T(128)} %bitcast.120), kind=kLoop, calls=%fused_computation.1.clone.1 | loop fusion | flops 63 | bytes 391 | tf_op jit(solution)/shard_map/vmap(vmap())/scatter
  114.8 2.2 %pad_maximum_fusion = bf16[2,382,1024]{1,2,0:T(8,128)(2,1)S(1)} fusion(bf16[2,63,1024]{1,2,0:T(8,128)(2,1)} %collective-permute-done.3, bf16[2,256,1024]{1,2,0:T(8,128)(2,1)S(1)} %fusion.3, bf16[2,63,1024]{1,2,0:T(8,128)(2,1)} %copy-done.3), kind=kLoop, calls=%fused_computation.26 | loop fusion | flops 4694016 | bytes 3129344 | tf_op jit(solution)/shard_map/concatenate | solution.py:23
  118.4 2.9 %copy.48 = bf16[2,382,8,128]{3,2,1,0:T(8,128)(2,1)} copy(bf16[2,382,8,128]{1,3,2,0:T(8,128)(2,1)} %bitcast.137) | data formatting | bytes 3129344 | tf_op jit(solution)/shard_map/reshape | solution.py:44
  121.4 2.0 %copy.50 = bf16[2,382,8,128]{3,2,1,0:T(8,128)(2,1)} copy(bf16[2,382,8,128]{1,3,2,0:T(8,128)(2,1)S(1)} %bitcast.136) | data formatting | bytes 3129344 | tf_op jit(solution)/shard_map/reshape | solution.py:44
  123.4 3.7 %fusion.28 = f32[2,382,8,128]{3,2,1,0:T(8,128)} fusion(bf16[2,382,8,128]{3,2,1,0:T(8,128)(2,1)} %copy.48, bf16[2,128,384]{2,1,0:T(8,128)(2,1)S(1)} %bitcast.139), kind=kOutput, calls=%fused_computation.61 | convolution fusion | flops 200278016 | bytes 4759552 | tf_op jit(solution)/shard_map/srny,scy->srnc/dot_general | solution.py:48
  127.1 2.2 %fusion.27 = f32[2,382,8,128]{3,2,1,0:T(8,128)} fusion(bf16[2,382,8,128]{3,2,1,0:T(8,128)(2,1)S(1)} %copy-done.1, bf16[2,128,384]{2,1,0:T(8,128)(2,1)S(1)} %bitcast.140), kind=kOutput, calls=%fused_computation.58 | convolution fusion | flops 200278016 | bytes 4759552 | tf_op jit(solution)/shard_map/srny,scy->srnc/dot_general | solution.py:48
  130.6 4.7 %add_convert_fusion = bf16[2,382,8,128]{3,2,1,0:T(8,128)(2,1)} fusion(f32[2,382,8,128]{3,2,1,0:T(8,128)} %fusion.27, f32[2,382,8,128]{3,2,1,0:T(8,128)} %fusion.28, bf16[2,382,8,128]{3,2,1,0:T(8,128)(2,1)S(1)} %copy.49, bf16[2,128,384]{2,1,0:T(8,128)(2,1)S(1)} %bitcast.141), kind=kOutput, calls=%fused_computation.14 | convolution fusion | flops 202625024 | bytes 9453568 | tf_op jit(solution)/shard_map/srny,scy->srnc/dot_general | solution.py:48
  135.2 2.1 %copy.51 = bf16[2,382,8,128]{1,3,2,0:T(8,128)(2,1)S(1)} copy(bf16[2,382,8,128]{3,2,1,0:T(8,128)(2,1)} %add_convert_fusion) | data formatting | bytes 3129344 | tf_op jit(solution)/shard_map/convert_element_type | solution.py:113
  139.7 48.7 %reduce-scatter.4.cloned.1.call-done = bf16[128,256]{1,0:T(8,128)(2,1)} async-done(((bf16[1024,256]{1,0:T(8,128)(2,1)}), bf16[128,256]{1,0:T(8,128)(2,1)}) %reduce-scatter.4.cloned.1.call-update) | async-done | bytes 65552
  (104 shorter events, 38.0 us)
Async XLA Ops:
  6.5 34.5 %copy-start = (s32[16,2]{0,1:T(2,128)S(1)}, s32[16,2]{0,1:T(2,128)}, u32[]{:S(2)}) copy-start(s32[16,2]{0,1:T(2,128)} %param.11) | copy-start | bytes 388
  6.5 80.1 %copy-start.2 = (bf16[256,1024]{1,0:T(8,128)(2,1)S(1)}, bf16[256,1024]{1,0:T(8,128)(2,1)}, u32[]{:S(2)}) copy-start(bf16[256,1024]{1,0:T(8,128)(2,1)} %param.9) | copy-start | bytes 1572868
  6.5 181.9 %reduce-scatter.4.cloned.1.call-start = ((), (), s32[]{:S(2)}) async-start(), calls=%async_computation.1 | async-start | bytes 589824
  33.0 54.0 %collective-permute-start = (bf16[63,1024]{1,0:T(8,128)(2,1)S(1)}, bf16[63,1024]{1,0:T(8,128)(2,1)S(1)}, u32[]{:S(2)}, u32[]{:S(2)}) collective-permute-start(bf16[63,1024]{1,0:T(8,128)(2,1)S(1)} %get-tuple-element.85), channel_id=1, source_target_pairs={{0,8},{8,16},{16,24},{24,32},{32,40},{40,48},{48,56},{56,64},{64,7... | collective-permute-start | bytes 387080 | tf_op jit(solution)/shard_map/ppermute | solution.py:21
  34.9 52.6 %collective-permute-start.1 = (bf16[63,1024]{1,0:T(8,128)(2,1)S(1)}, bf16[63,1024]{1,0:T(8,128)(2,1)S(1)}, u32[]{:S(2)}, u32[]{:S(2)}) collective-permute-start(bf16[63,1024]{1,0:T(8,128)(2,1)S(1)} %get-tuple-element.86), channel_id=1, source_target_pairs={{8,0},{16,8},{24,16},{32,24},{40,32},{48,40},{56,48},{64,56},{72,6... | collective-permute-start | bytes 387080 | tf_op jit(solution)/shard_map/ppermute | solution.py:22
  71.0 15.8 %copy-start.7 = (f32[4]{0:T(128)S(1)}, f32[4]{0:T(128)}, u32[]{:S(2)}) copy-start(f32[4]{0:T(128)} %param.13) | copy-start | bytes 52
  90.2 9.2 %copy-start.6 = (s32[2]{0:T(128)S(1)}, s32[2]{0:T(128)}, u32[]{:S(2)}) copy-start(s32[2]{0:T(128)} %get-tuple-element.297) | copy-start | bytes 28
  91.3 22.7 %collective-permute-start.2 = (bf16[2,63,1024]{1,2,0:T(8,128)(2,1)}, bf16[2,63,1024]{1,2,0:T(8,128)(2,1)S(1)}, u32[]{:S(2)}, u32[]{:S(2)}) collective-permute-start(bf16[2,63,1024]{1,2,0:T(8,128)(2,1)} %get-tuple-element.83), channel_id=1, source_target_pairs={{0,8},{8,16},{16,24},{24,32},{32,40},{40,48},{48,56},{56,64},{64,7... | collective-permute-start | bytes 774152 | tf_op jit(solution)/shard_map/ppermute | solution.py:21
  93.2 21.6 %collective-permute-start.3 = (bf16[2,63,1024]{1,2,0:T(8,128)(2,1)S(1)}, bf16[2,63,1024]{1,2,0:T(8,128)(2,1)}, u32[]{:S(2)}, u32[]{:S(2)}) collective-permute-start(bf16[2,63,1024]{1,2,0:T(8,128)(2,1)S(1)} %get-tuple-element.84), channel_id=1, source_target_pairs={{8,0},{16,8},{24,16},{32,24},{40,32},{48,40},{56,48},{64,56},{72,6... | collective-permute-start | bytes 774152 | tf_op jit(solution)/shard_map/ppermute | solution.py:22
  114.0 0.8 copy-start.3
  123.4 3.7 %copy-start.1 = (bf16[2,382,8,128]{3,2,1,0:T(8,128)(2,1)S(1)}, bf16[2,382,8,128]{3,2,1,0:T(8,128)(2,1)}, u32[]{:S(2)}) copy-start(bf16[2,382,8,128]{3,2,1,0:T(8,128)(2,1)} %copy.50) | copy-start | bytes 4694020
  138.3 51.1 %copy-start.4 = (bf16[256,128]{1,0:T(8,128)(2,1)S(1)}, bf16[256,128]{1,0:T(8,128)(2,1)}, u32[]{:S(2)}) copy-start(bf16[256,128]{1,0:T(8,128)(2,1)} %param.8) | copy-start | bytes 196612
  138.3 51.1 %copy-start.5 = (s32[256,128]{1,0:T(8,128)S(1)}, s32[256,128]{1,0:T(8,128)}, u32[]{:S(2)}) copy-start(s32[256,128]{1,0:T(8,128)} %param.10) | copy-start | bytes 393220
Sparse Core Ops, SparseCore 0:
  139.8 48.5 reduce-scatter.3
where the time goes:
time: 198 us; the launch traced here: 197 us
  waiting for transfers between devices  48.8 us (25%)
  other arithmetic  41.2 us (21%)
  local copies, waits for them, and re-layouts  36.8 us (19%)
  blocking collectives  26.4 us (13%)
  starting transfers between devices  16.1 us (8%)
  between operations  13.8 us (7%)
  matrix products  13.6 us (7%)
    unnamed x2, waiting for transfers between devices  48.7 us
    scatter x16, other arithmetic  35.7 us
    all_gather x1, blocking collectives, shards(): full_map = lax.all_gather(dwell_map, 'scen', axis=1, tiled=True)  26.4 us
    scatter x24, local copies, waits for them, and re-layouts  17.4 us
    ppermute x2, starting transfers between devices, extended(): after = lax.ppermute(first, axis, down)  12.3 us
    dot_general x6, matrix products, column_pass(): jnp.einsum('srny,scy->srnc', view, part_mat, preferred_element_type=jnp.f...  12 us
    reshape x3, local copies, waits for them, and re-layouts, column_pass(): padded[:, :, piece * col_block:piece * col_block + col_total]  6.16 us
  transfers between devices with their start and end apart: 5, of which 1 were waited for; matrix products, arithmetic and copies ran while one was open for 31% of the time, Pallas kernels for 0%

commit v1 on v0

v1 whole, which is shorter than its diff:
```python
import functools

import jax
import jax.numpy as jnp
from jax import lax
from jax.experimental import pallas as pl
from jax.experimental.pallas import tpu as pltpu
from jax.sharding import PartitionSpec as P

MESH = pl.DeviceIdType.MESH
F32 = jnp.float32
BF16 = jnp.bfloat16

TAPS = 63
RADIUS = 31
ROWS = 256
COLS = 128
RIM = 64
RING = 256
OUT = 320
NRATE = 4
SCEN = 16
STEP_SIZE = 1.0
CHUNK = 16


def lanes(shape):
    return lax.broadcasted_iota(jnp.int32, shape, len(shape) - 1)


def kernel(
    n_space,
    n_scen,
    dwell_hbm,
    target_hbm,
    off_s,
    level_s,
    rate_s,
    off_v,
    level_v,
    row_taps,
    col_taps,
    grad_ref,
    dwell_x,
    pack_l,
    pack_r,
    recv_l,
    recv_r,
    t_own,
    t_top,
    t_bot,
    wide,
    taps8,
    row_fwd,
    col_mat,
    row_adj,
    count,
    t_sum,
    along,
    back,
    send_sem,
    recv_sem,
    load_sem,
):
    sp = lax.axis_index("space")
    sc = lax.axis_index("scen")
    up, down = (sp + n_space - 1) % n_space, (sp + 1) % n_space
    left, right = (sc + n_scen - 1) % n_scen, (sc + 1) % n_scen
    core = sp % 2
    other = (sc + n_scen // 2) % n_scen
    up_sc = jnp.where(core == 0, other, sc)
    down_sc = jnp.where(core == 0, sc, other)

    def first_tile(c):
        return jnp.minimum(jnp.maximum(c - 1, 0), n_scen - 3)

    def window(c):
        return pl.ds(pl.multiple_of(first_tile(c) * COLS, COLS), 3 * COLS)

    peers = (
        (up, sc),
        (down, sc),
        (sp, left),
        (sp, right),
        (up, left),
        (up, right),
        (down, left),
        (down, right),
        (up, up_sc),
        (down, down_sc),
    )
    barrier = pltpu.get_barrier_semaphore()
    for peer in peers:
        pl.semaphore_signal(barrier, inc=1, device_id=peer, device_id_type=MESH)

    load_dwell = pltpu.make_async_copy(
        dwell_hbm, dwell_x.at[RIM : RIM + ROWS, 0:COLS], load_sem.at[0]
    )
    load_target = pltpu.make_async_copy(target_hbm.at[:, window(sc)], t_own, load_sem.at[1])
    load_dwell.start()
    load_target.start()
    load_dwell.wait()

    low = lanes((32, COLS)) < RIM
    for g in range(4):
        base = RIM + 64 * g
        first = dwell_x[base : base + 32, 0:COLS].astype(F32)
        second = pltpu.roll(dwell_x[base + 32 : base + 64, 0:COLS].astype(F32), RIM, 1)
        pack_l[32 * g : 32 * g + 32, :] = jnp.where(low, first, second).astype(BF16)
        pack_r[32 * g : 32 * g + 32, :] = jnp.where(low, second, first).astype(BF16)

    pl.semaphore_wait(barrier, len(peers))

    sides = (
        (pack_l, recv_r.at[32:160]),
        (pack_r, recv_l.at[32:160]),
        (pack_l.at[0:32], recv_r.at[160:192]),
        (pack_r.at[0:32], recv_l.at[160:192]),
        (pack_l.at[96:128], recv_r.at[0:32]),
        (pack_r.at[96:128], recv_l.at[0:32]),
    )
    pairs = (
        (dwell_hbm.at[0:RIM], dwell_x.at[RIM + ROWS : RIM + ROWS + RIM, 0:COLS]),
        (dwell_hbm.at[ROWS - RIM : ROWS], dwell_x.at[0:RIM, 0:COLS]),
        *sides,
        (target_hbm.at[0:RIM, window(up_sc)], t_bot),
        (target_hbm.at[ROWS - RIM : ROWS, window(down_sc)], t_top),
    )
    copies = [
        pltpu.make_async_remote_copy(
            src_ref=src,
            dst_ref=dst,
            send_sem=send_sem.at[k],
            recv_sem=recv_sem.at[k],
            device_id=peers[k],
            device_id_type=MESH,
        )
        for k, (src, dst) in enumerate(pairs)
    ]
    for k in (2, 3, 4, 5, 6, 7, 0, 1, 8, 9):
        copies[k].start()

    has_up = jnp.where(sp > 0, 1.0, 0.0).astype(F32)
    has_down = jnp.where(sp < n_space - 1, 1.0, 0.0).astype(F32)
    has_left = jnp.where(sc > 0, 1.0, 0.0).astype(F32)
    has_right = jnp.where(sc < n_scen - 1, 1.0, 0.0).astype(F32)

    taps8[...] = jnp.zeros_like(taps8)
    taps8[0:NRATE, 0:TAPS] = row_taps[...].astype(F32)
    taps8[4 : 4 + NRATE, 0:TAPS] = col_taps[...].astype(F32)
    taps = taps8[...]
    flip = jnp.where(
        lax.broadcasted_iota(jnp.int32, (RING, RING), 0) + lanes((RING, RING)) == TAPS - 1, 1.0, 0.0
    ).astype(BF16)
    reversed_taps = jnp.dot(taps.astype(BF16), flip, preferred_element_type=F32)

    def toeplitz(line, count_, first):
        return pltpu.roll(
            jnp.broadcast_to(line, (count_, RING)), first % RING, 1, stride=1, stride_axis=0
        ).astype(BF16)

    for q in range(NRATE):
        row_fwd[0, 160 * q : 160 * q + 160, :] = toeplitz(taps[q : q + 1], 160, 1)
        row_fwd[1, 160 * q : 160 * q + 160, :] = toeplitz(taps[q : q + 1], 160, 33)
        col_mat[q] = toeplitz(taps[4 + q : 5 + q], RING, -RADIUS)
        row_adj[:, RING * q : RING * q + RING] = toeplitz(reversed_taps[q : q + 1], 128, 1)

    offs = off_v[...]
    row_at = sp * ROWS + lax.broadcasted_iota(jnp.int32, (OUT, SCEN), 0) - 32 + offs[0:1, :]
    row_in = jnp.where((row_at >= 0) & (row_at < n_space * ROWS), 1.0, 0.0).astype(BF16)
    ring_at = lax.broadcasted_iota(jnp.int32, (RING, SCEN), 0)
    col_at = jnp.where(ring_at < COLS + RIM, ring_at, ring_at - RING) + sc * COLS + offs[1:2, :]
    col_in = jnp.where((col_at >= 0) & (col_at < n_scen * COLS), 1.0, 0.0)
    levels = level_v[...]
    for q in range(NRATE):
        mine = jnp.where(levels == q, 1.0, 0.0)
        seen = lax.dot_general(
            row_in, (col_in * mine).astype(BF16), (((1,), (1,)), ((), ())), preferred_element_type=F32
        )
        rate = rate_s[q]
        count[q] = seen * (rate * rate * (1.0 / SCEN))

    at = sc - first_tile(sc)
    ring_low = lanes((1, COLS)) < RIM
    side_ok = jnp.where(ring_low, has_right, has_left)

    def to_ring(ref, rows):
        own = ref[rows, pl.ds(pl.multiple_of(at * COLS, COLS), COLS)].astype(F32)
        after = ref[rows, pl.ds(pl.multiple_of(jnp.minimum(at + 1, 2) * COLS, COLS), COLS)].astype(F32)
        before = ref[rows, pl.ds(pl.multiple_of(jnp.maximum(at - 1, 0) * COLS, COLS), COLS)].astype(F32)
        return own, jnp.where(ring_low, after, before) * side_ok

    load_target.wait()
    own, side = to_ring(t_own, slice(0, ROWS))
    wide[0, RIM : RIM + ROWS, :] = own
    wide[1, RIM : RIM + ROWS, :] = side

    shift_rows = [off_s[0, s] for s in range(SCEN)]
    shift_cols = [lax.rem(RING - off_s[1, s], RING) for s in range(SCEN)]
    weights = [
        [jnp.where(level_s[0, s] == q, rate_s[q] * (1.0 / SCEN), 0.0) for q in range(NRATE)]
        for s in range(SCEN)
    ]

    def target_rows(c, carry):
        begin = c * CHUNK
        sums = [jnp.zeros((CHUNK, RING), F32) for _ in range(NRATE)]
        for s in range(SCEN):
            start = begin + 32 + shift_rows[s]
            part = jnp.concatenate([wide[side_, pl.ds(start, CHUNK), :] for side_ in range(2)], axis=1)
            part = pltpu.roll(part, shift_cols[s], 1)
            sums = [acc + weights[s][q] * part for q, acc in enumerate(sums)]
        for q in range(NRATE):
            t_sum[q, pl.ds(pl.multiple_of(begin, CHUNK), CHUNK), :] = sums[q]
        return carry

    lax.fori_loop(64 // CHUNK, 256 // CHUNK, target_rows, 0)

    for copy in copies[8:]:
        copy.wait()
    own, side = to_ring(t_top, slice(0, RIM))
    wide[0, 0:RIM, :] = own * has_up
    wide[1, 0:RIM, :] = side * has_up
    own, side = to_ring(t_bot, slice(0, RIM))
    wide[0, RIM + ROWS :, :] = own * has_down
    wide[1, RIM + ROWS :, :] = side * has_down
    lax.fori_loop(0, 64 // CHUNK, target_rows, 0)
    lax.fori_loop(256 // CHUNK, OUT // CHUNK, target_rows, 0)

    for copy in copies[:8]:
        copy.wait()

    dwell_x[0:RIM, 0:COLS] = (dwell_x[0:RIM, 0:COLS].astype(F32) * has_up).astype(BF16)
    dwell_x[RIM + ROWS :, 0:COLS] = (dwell_x[RIM + ROWS :, 0:COLS].astype(F32) * has_down).astype(BF16)
    for g in range(6):
        ok = side_ok
        if g == 0:
            ok = ok * has_up
        if g == 5:
            ok = ok * has_down
        after = recv_r[32 * g : 32 * g + 32, :].astype(F32)
        before = recv_l[32 * g : 32 * g + 32, :].astype(F32)
        first = jnp.where(low, after, before) * ok
        second = pltpu.roll(jnp.where(low, before, after), RIM, 1) * ok
        dwell_x[64 * g : 64 * g + 32, COLS:RING] = first.astype(BF16)
        dwell_x[64 * g + 32 : 64 * g + 64, COLS:RING] = second.astype(BF16)

    for half in range(2):
        product = jnp.dot(
            row_fwd[half], dwell_x[128 * half : 128 * half + 256, :], preferred_element_type=F32
        ).astype(BF16)
        for q in range(NRATE):
            along[q, 160 * half : 160 * half + 160, :] = product[160 * q : 160 * q + 160]

    for q in range(NRATE):
        base = lax.dot_general(
            along[q], col_mat[q], (((1,), (1,)), ((), ())), preferred_element_type=F32
        )
        misfit = (count[q] * base - t_sum[q]).astype(BF16)
        product = jnp.dot(misfit, col_mat[q, :, 0:COLS], preferred_element_type=F32).astype(BF16)
        back[RING * q : RING * q + 256, 0:COLS] = product[0:256]
        back[RING * q : RING * q + 192, COLS:RING] = product[128:OUT]
        back[RING * q + 192 : RING * q + 256, COLS:RING] = jnp.zeros((64, COLS), BF16)

    grad = jnp.dot(row_adj[...], back[...], preferred_element_type=F32)
    grad_ref[0:128, :] = grad[:, 0:COLS]
    grad_ref[128:256, :] = grad[:, COLS:RING]


def tile_step(n_space, n_scen, dwell, target, bound, offsets, level, rates, row_kernels, col_kernels):
    offsets, level = offsets.T, level.T
    vmem = pl.BlockSpec(memory_space=pltpu.VMEM)
    smem = pl.BlockSpec(memory_space=pltpu.SMEM)
    far = pl.BlockSpec(memory_space=pltpu.HBM)
    gradient = pl.pallas_call(
        functools.partial(kernel, n_space, n_scen),
        out_shape=jax.ShapeDtypeStruct((ROWS, COLS), F32),
        in_specs=[far, far, smem, smem, smem, vmem, vmem, vmem, vmem],
        out_specs=vmem,
        scratch_shapes=[
            pltpu.VMEM((384, RING), BF16),
            pltpu.VMEM((128, COLS), BF16),
            pltpu.VMEM((128, COLS), BF16),
            pltpu.VMEM((192, COLS), BF16),
            pltpu.VMEM((192, COLS), BF16),
            pltpu.VMEM((ROWS, 3 * COLS), BF16),
            pltpu.VMEM((RIM, 3 * COLS), BF16),
            pltpu.VMEM((RIM, 3 * COLS), BF16),
            pltpu.VMEM((2, 384, COLS), F32),
            pltpu.VMEM((8, RING), F32),
            pltpu.VMEM((2, NRATE * 160, RING), BF16),
            pltpu.VMEM((NRATE, RING, RING), BF16),
            pltpu.VMEM((128, NRATE * RING), BF16),
            pltpu.VMEM((NRATE, OUT, RING), F32),
            pltpu.VMEM((NRATE, OUT, RING), F32),
            pltpu.VMEM((NRATE, OUT, RING), BF16),
            pltpu.VMEM((NRATE * RING, RING), BF16),
            pltpu.SemaphoreType.DMA((10,)),
            pltpu.SemaphoreType.DMA((10,)),
            pltpu.SemaphoreType.DMA((2,)),
        ],
        compiler_params=pltpu.CompilerParams(collective_id=0, vmem_limit_bytes=63 * 1024 * 1024),
    )(dwell, target, offsets, level, rates, offsets, level, row_kernels, col_kernels)
    stepped = dwell.astype(F32) - STEP_SIZE * gradient
    return jnp.where(bound == 1, jnp.maximum(stepped, 0.0), stepped).astype(BF16)


def solution(mesh):
    return jax.shard_map(
        functools.partial(tile_step, mesh.shape["space"], mesh.shape["scen"]),
        mesh=mesh,
        in_specs=(P("space", "scen"), P("space", None), P("space", "scen"), P(), P(), P(), P(), P()),
        out_specs=P("space", "scen"),
        check_vma=False,
    )
```

time: 198 us -> 23.1 us (0.12)
  the two profiles are of different devices: /device:TPU:32 before, /device:TPU:1 now
where the time goes in v1:
time: 23.1 us; the launch traced here: 23 us
  Pallas kernels  21.4 us (93%)
  other arithmetic  1.56 us (7%)
    pallas_call x1, Pallas kernels, tile_step(): pl.pallas_call(functools.partial(kernel, n_space, n_scen), out_shape=jax....  21.4 us
    convert_element_type x1, other arithmetic, tile_step(): jnp.where(bound == 1, jnp.maximum(stepped, 0.0), stepped).astype(BF16)  1.56 us

profile of v1, /device:TPU:1, one launch (start us, length us, event | category | flops | bytes accessed | tf_op | source)
XLA Modules:
  0.0 23.0 jit_solution(6316216907508644148)
XLA Ops:
  0.0 0.0 copy-start
  0.0 0.0 copy-start.1
  0.0 21.4 %shard_map.82 = f32[256,128]{1,0:T(8,128)} custom-call(bf16[256,128]{1,0:T(8,128)(2,1)} %dwell_hbm.1, bf16[256,1024]{1,0:T(8,128)(2,1)} %target_hbm.1, s32[2,16]{1,0:T(2,128)} %bitcast.2, s32[1,16]{1,0:T(1,128)} %bitcast.4, f32[4]{0:T(128)} %rate_s.1, s32[2,16]{1,0:T(2,128)} %bitcast.3, s32[1,16]{1,0:T(1,128)} %bitcast.5, bf16[4,63]{1,0:T(4,128)(2,1)} %row_taps.1, ...), custom_call_target="tpu_custom_call" | custom-call | tf_op jit(solution)/shard_map/pallas_call | solution.py:275
  21.4 0.0 copy-done
  21.4 0.0 copy-done.1
  21.4 1.6 %fusion = bf16[256,128]{1,0:T(8,128)(2,1)} fusion(f32[256,128]{1,0:T(8,128)} %shard_map.82, bf16[256,128]{1,0:T(8,128)(2,1)S(1)} %copy-done, s32[256,128]{1,0:T(8,128)S(1)} %copy-done.1), kind=kLoop, calls=%fused_computation.1 | loop fusion | flops 196608 | bytes 393216 | tf_op jit(solution)/shard_map/convert_element_type | solution.py:305
Async XLA Ops:
  0.0 21.4 %copy-start = (bf16[256,128]{1,0:T(8,128)(2,1)S(1)}, bf16[256,128]{1,0:T(8,128)(2,1)}, u32[]{:S(2)}) copy-start(bf16[256,128]{1,0:T(8,128)(2,1)} %dwell_hbm.1) | copy-start | bytes 196612
  0.0 21.4 %copy-start.1 = (s32[256,128]{1,0:T(8,128)S(1)}, s32[256,128]{1,0:T(8,128)}, u32[]{:S(2)}) copy-start(s32[256,128]{1,0:T(8,128)} %param.10) | copy-start | bytes 393220

commit v2 on v1

--- a/solution.py
+++ b/solution.py
@@ -33,6 +33,12 @@
     n_scen,
     dwell_hbm,
     target_hbm,
+    off_hbm,
+    level_hbm,
+    rate_hbm,
+    row_hbm,
+    col_hbm,
+    grad_ref,
     off_s,
     level_s,
     rate_s,
@@ -40,12 +46,12 @@
     level_v,
     row_taps,
     col_taps,
-    grad_ref,
     dwell_x,
     pack_l,
     pack_r,
     recv_l,
     recv_r,
+    corners,
     t_own,
     t_top,
     t_bot,
@@ -64,8 +70,9 @@
 ):
     sp = lax.axis_index("space")
     sc = lax.axis_index("scen")
-    up, down = (sp + n_space - 1) % n_space, (sp + 1) % n_space
-    left, right = (sc + n_scen - 1) % n_scen, (sc + 1) % n_scen
+    up, down, left, right = sp - 1, sp + 1, sc - 1, sc + 1
+    has_up, has_down = sp > 0, sp < n_space - 1
+    has_left, has_right = sc > 0, sc < n_scen - 1
     core = sp % 2
     other = (sc + n_scen // 2) % n_scen
     up_sc = jnp.where(core == 0, other, sc)
@@ -78,30 +85,52 @@
         return pl.ds(pl.multiple_of(first_tile(c) * COLS, COLS), 3 * COLS)
 
     peers = (
-        (up, sc),
-        (down, sc),
-        (sp, left),
-        (sp, right),
-        (up, left),
-        (up, right),
-        (down, left),
-        (down, right),
-        (up, up_sc),
-        (down, down_sc),
+        (up, sc, has_up),
+        (down, sc, has_down),
+        (sp, left, has_left),
+        (sp, right, has_right),
+        (up, left, has_up & has_left),
+        (up, right, has_up & has_right),
+        (down, left, has_down & has_left),
+        (down, right, has_down & has_right),
+        (up, up_sc, has_up),
+        (down, down_sc, has_down),
     )
+    comes = [peers[k][2] for k in (1, 0, 3, 2, 7, 6, 5, 4, 9, 8)]
     barrier = pltpu.get_barrier_semaphore()
-    for peer in peers:
-        pl.semaphore_signal(barrier, inc=1, device_id=peer, device_id_type=MESH)
+    for row, col, there in peers:
+
+        @pl.when(there)
+        def _(row=row, col=col):
+            pl.semaphore_signal(barrier, inc=1, device_id=(row, col), device_id_type=MESH)
+
+    greeted = sum(jnp.where(there, 1, 0) for _, _, there in peers)
 
     load_dwell = pltpu.make_async_copy(
         dwell_hbm, dwell_x.at[RIM : RIM + ROWS, 0:COLS], load_sem.at[0]
     )
     load_target = pltpu.make_async_copy(target_hbm.at[:, window(sc)], t_own, load_sem.at[1])
     load_dwell.start()
+    small = [
+        pltpu.make_async_copy(src, dst, load_sem.at[2 + k])
+        for k, (src, dst) in enumerate(
+            (
+                (row_hbm, row_taps),
+                (col_hbm, col_taps),
+                (rate_hbm, rate_s),
+                (off_hbm, off_v),
+                (level_hbm, level_v),
+                (off_hbm, off_s),
+                (level_hbm, level_s),
+            )
+        )
+    ]
+    for load in small:
+        load.start()
     load_target.start()
     load_dwell.wait()
 
-    low = lanes((32, COLS)) < RIM
+    low = lanes((1, COLS)) < RIM
     for g in range(4):
         base = RIM + 64 * g
         first = dwell_x[base : base + 32, 0:COLS].astype(F32)
@@ -109,22 +138,20 @@
         pack_l[32 * g : 32 * g + 32, :] = jnp.where(low, first, second).astype(BF16)
         pack_r[32 * g : 32 * g + 32, :] = jnp.where(low, second, first).astype(BF16)
 
-    pl.semaphore_wait(barrier, len(peers))
-
-    sides = (
-        (pack_l, recv_r.at[32:160]),
-        (pack_r, recv_l.at[32:160]),
-        (pack_l.at[0:32], recv_r.at[160:192]),
-        (pack_r.at[0:32], recv_l.at[160:192]),
-        (pack_l.at[96:128], recv_r.at[0:32]),
-        (pack_r.at[96:128], recv_l.at[0:32]),
-    )
+    pl.semaphore_wait(barrier, greeted)
+
+    first_rows, last_rows = slice(0, RIM), slice(ROWS - RIM, ROWS)
     pairs = (
-        (dwell_hbm.at[0:RIM], dwell_x.at[RIM + ROWS : RIM + ROWS + RIM, 0:COLS]),
-        (dwell_hbm.at[ROWS - RIM : ROWS], dwell_x.at[0:RIM, 0:COLS]),
-        *sides,
-        (target_hbm.at[0:RIM, window(up_sc)], t_bot),
-        (target_hbm.at[ROWS - RIM : ROWS, window(down_sc)], t_top),
+        (dwell_hbm.at[first_rows], dwell_x.at[RIM + ROWS : RIM + ROWS + RIM, 0:COLS]),
+        (dwell_hbm.at[last_rows], dwell_x.at[0:RIM, 0:COLS]),
+        (pack_l, recv_r),
+        (pack_r, recv_l),
+        (dwell_hbm.at[first_rows], corners.at[3]),
+        (dwell_hbm.at[first_rows], corners.at[2]),
+        (dwell_hbm.at[last_rows], corners.at[1]),
+        (dwell_hbm.at[last_rows], corners.at[0]),
+        (target_hbm.at[first_rows, window(up_sc)], t_bot),
+        (target_hbm.at[last_rows, window(down_sc)], t_top),
     )
     copies = [
         pltpu.make_async_remote_copy(
@@ -132,18 +159,23 @@
             dst_ref=dst,
             send_sem=send_sem.at[k],
             recv_sem=recv_sem.at[k],
-            device_id=peers[k],
+            device_id=peers[k][:2],
             device_id_type=MESH,
         )
         for k, (src, dst) in enumerate(pairs)
     ]
-    for k in (2, 3, 4, 5, 6, 7, 0, 1, 8, 9):
-        copies[k].start()
-
-    has_up = jnp.where(sp > 0, 1.0, 0.0).astype(F32)
-    has_down = jnp.where(sp < n_space - 1, 1.0, 0.0).astype(F32)
-    has_left = jnp.where(sc > 0, 1.0, 0.0).astype(F32)
-    has_right = jnp.where(sc < n_scen - 1, 1.0, 0.0).astype(F32)
+    for k in (4, 5, 6, 7, 0, 1, 2, 3, 8, 9):
+        pl.when(peers[k][2])(copies[k].start)
+
+    def arrive(ks):
+        for k in ks:
+            pl.when(comes[k])(copies[k].wait_recv)
+
+    side_ok = jnp.where(lanes((1, COLS)) < RIM, jnp.where(has_right, 1, 0), jnp.where(has_left, 1, 0)) > 0
+    low = lanes((1, COLS)) < RIM
+
+    for load in small:
+        load.wait()
 
     taps8[...] = jnp.zeros_like(taps8)
     taps8[0:NRATE, 0:TAPS] = row_taps[...].astype(F32)
@@ -181,14 +213,12 @@
         count[q] = seen * (rate * rate * (1.0 / SCEN))
 
     at = sc - first_tile(sc)
-    ring_low = lanes((1, COLS)) < RIM
-    side_ok = jnp.where(ring_low, has_right, has_left)
 
     def to_ring(ref, rows):
         own = ref[rows, pl.ds(pl.multiple_of(at * COLS, COLS), COLS)].astype(F32)
         after = ref[rows, pl.ds(pl.multiple_of(jnp.minimum(at + 1, 2) * COLS, COLS), COLS)].astype(F32)
         before = ref[rows, pl.ds(pl.multiple_of(jnp.maximum(at - 1, 0) * COLS, COLS), COLS)].astype(F32)
-        return own, jnp.where(ring_low, after, before) * side_ok
+        return own, jnp.where(side_ok, jnp.where(low, after, before), 0.0)
 
     load_target.wait()
     own, side = to_ring(t_own, slice(0, ROWS))
@@ -216,34 +246,34 @@
 
     lax.fori_loop(64 // CHUNK, 256 // CHUNK, target_rows, 0)
 
-    for copy in copies[8:]:
-        copy.wait()
+    arrive((8, 9))
     own, side = to_ring(t_top, slice(0, RIM))
-    wide[0, 0:RIM, :] = own * has_up
-    wide[1, 0:RIM, :] = side * has_up
+    wide[0, 0:RIM, :] = jnp.where(has_up, own, 0.0)
+    wide[1, 0:RIM, :] = jnp.where(has_up, side, 0.0)
     own, side = to_ring(t_bot, slice(0, RIM))
-    wide[0, RIM + ROWS :, :] = own * has_down
-    wide[1, RIM + ROWS :, :] = side * has_down
+    wide[0, RIM + ROWS :, :] = jnp.where(has_down, own, 0.0)
+    wide[1, RIM + ROWS :, :] = jnp.where(has_down, side, 0.0)
     lax.fori_loop(0, 64 // CHUNK, target_rows, 0)
     lax.fori_loop(256 // CHUNK, OUT // CHUNK, target_rows, 0)
 
-    for copy in copies[:8]:
-        copy.wait()
-
-    dwell_x[0:RIM, 0:COLS] = (dwell_x[0:RIM, 0:COLS].astype(F32) * has_up).astype(BF16)
-    dwell_x[RIM + ROWS :, 0:COLS] = (dwell_x[RIM + ROWS :, 0:COLS].astype(F32) * has_down).astype(BF16)
-    for g in range(6):
-        ok = side_ok
-        if g == 0:
-            ok = ok * has_up
-        if g == 5:
-            ok = ok * has_down
+    arrive(range(8))
+
+    def corner(before, after, there):
+        x = jnp.where(low, corners[after].astype(F32), corners[before].astype(F32))
+        return jnp.where(there, jnp.where(side_ok, x, 0.0), 0.0).astype(BF16)
+
+    dwell_x[0:RIM, 0:COLS] = jnp.where(has_up, dwell_x[0:RIM, 0:COLS].astype(F32), 0.0).astype(BF16)
+    dwell_x[RIM + ROWS :, 0:COLS] = jnp.where(has_down, dwell_x[RIM + ROWS :, 0:COLS].astype(F32), 0.0).astype(BF16)
+    dwell_x[0:RIM, COLS:RING] = corner(0, 1, has_up)
+    dwell_x[RIM + ROWS :, COLS:RING] = corner(2, 3, has_down)
+    for g in range(4):
         after = recv_r[32 * g : 32 * g + 32, :].astype(F32)
         before = recv_l[32 * g : 32 * g + 32, :].astype(F32)
-        first = jnp.where(low, after, before) * ok
-        second = pltpu.roll(jnp.where(low, before, after), RIM, 1) * ok
-        dwell_x[64 * g : 64 * g + 32, COLS:RING] = first.astype(BF16)
-        dwell_x[64 * g + 32 : 64 * g + 64, COLS:RING] = second.astype(BF16)
+        first = jnp.where(side_ok, jnp.where(low, after, before), 0.0)
+        second = jnp.where(side_ok, pltpu.roll(jnp.where(low, before, after), RIM, 1), 0.0)
+        base = RIM + 64 * g
+        dwell_x[base : base + 32, COLS:RING] = first.astype(BF16)
+        dwell_x[base + 32 : base + 64, COLS:RING] = second.astype(BF16)
 
     for half in range(2):
         product = jnp.dot(
@@ -265,24 +295,33 @@
     grad = jnp.dot(row_adj[...], back[...], preferred_element_type=F32)
     grad_ref[0:128, :] = grad[:, 0:COLS]
     grad_ref[128:256, :] = grad[:, COLS:RING]
+    for k in range(10):
+        pl.when(peers[k][2])(copies[k].wait_send)
 
 
 def tile_step(n_space, n_scen, dwell, target, bound, offsets, level, rates, row_kernels, col_kernels):
     offsets, level = offsets.T, level.T
     vmem = pl.BlockSpec(memory_space=pltpu.VMEM)
-    smem = pl.BlockSpec(memory_space=pltpu.SMEM)
     far = pl.BlockSpec(memory_space=pltpu.HBM)
     gradient = pl.pallas_call(
         functools.partial(kernel, n_space, n_scen),
         out_shape=jax.ShapeDtypeStruct((ROWS, COLS), F32),
-        in_specs=[far, far, smem, smem, smem, vmem, vmem, vmem, vmem],
+        in_specs=[far] * 7,
         out_specs=vmem,
         scratch_shapes=[
+            pltpu.SMEM((2, SCEN), jnp.int32),
+            pltpu.SMEM((1, SCEN), jnp.int32),
+            pltpu.SMEM((NRATE,), F32),
+            pltpu.VMEM((2, SCEN), jnp.int32),
+            pltpu.VMEM((1, SCEN), jnp.int32),
+            pltpu.VMEM((NRATE, TAPS), BF16),
+            pltpu.VMEM((NRATE, TAPS), BF16),
             pltpu.VMEM((384, RING), BF16),
             pltpu.VMEM((128, COLS), BF16),
             pltpu.VMEM((128, COLS), BF16),
-            pltpu.VMEM((192, COLS), BF16),
-            pltpu.VMEM((192, COLS), BF16),
+            pltpu.VMEM((128, COLS), BF16),
+            pltpu.VMEM((128, COLS), BF16),
+            pltpu.VMEM((4, RIM, COLS), BF16),
             pltpu.VMEM((ROWS, 3 * COLS), BF16),
             pltpu.VMEM((RIM, 3 * COLS), BF16),
             pltpu.VMEM((RIM, 3 * COLS), BF16),
@@ -297,10 +336,10 @@
             pltpu.VMEM((NRATE * RING, RING), BF16),
             pltpu.SemaphoreType.DMA((10,)),
             pltpu.SemaphoreType.DMA((10,)),
-            pltpu.SemaphoreType.DMA((2,)),
+            pltpu.SemaphoreType.DMA((9,)),
         ],
         compiler_params=pltpu.CompilerParams(collective_id=0, vmem_limit_bytes=63 * 1024 * 1024),
-    )(dwell, target, offsets, level, rates, offsets, level, row_kernels, col_kernels)
+    )(dwell, target, offsets, level, rates, row_kernels, col_kernels)
     stepped = dwell.astype(F32) - STEP_SIZE * gradient
     return jnp.where(bound == 1, jnp.maximum(stepped, 0.0), stepped).astype(BF16)
 

time: 23.1 us -> 16.1 us (0.70)
  Pallas kernels: 21.4 us -> 14.3 us
    pallas_call x1, Pallas kernels: 21.4 us -> 14.3 us  [tile_step(): pl.pallas_call(functools.partial(kernel, n_space, n_scen), out_shape=jax....]
where the time goes in v2:
time: 16.1 us; the launch traced here: 15.9 us
  Pallas kernels  14.3 us (89%)
  other arithmetic  1.56 us (10%)
    pallas_call x1, Pallas kernels, tile_step(): pl.pallas_call(functools.partial(kernel, n_space, n_scen), out_shape=jax....  14.3 us
    convert_element_type x1, other arithmetic, tile_step(): jnp.where(bound == 1, jnp.maximum(stepped, 0.0), stepped).astype(BF16)  1.56 us

profile of v2, /device:TPU:1, one launch (start us, length us, event | category | flops | bytes accessed | tf_op | source)
XLA Modules:
  0.0 15.9 jit_solution(4242766688916509556)
XLA Ops:
  0.0 0.0 copy-start
  0.0 0.0 copy-start.1
  0.0 14.3 %shard_map.82 = f32[256,128]{1,0:T(8,128)} custom-call(bf16[256,128]{1,0:T(8,128)(2,1)} %dwell_hbm.1, bf16[256,1024]{1,0:T(8,128)(2,1)} %target_hbm.1, s32[2,16]{1,0:T(2,128)} %bitcast.2, s32[1,16]{1,0:T(1,128)} %bitcast.3, f32[4]{0:T(128)} %rate_hbm.1, bf16[4,63]{1,0:T(4,128)(2,1)} %row_hbm.1, bf16[4,63]{1,0:T(4,128)(2,1)} %col_hbm.1), custom_call_target="tpu_custom_call" | custom-call | tf_op jit(solution)/shard_map/pallas_call | solution.py:306
  14.4 0.0 copy-done
  14.4 0.0 copy-done.1
  14.4 1.6 %fusion = bf16[256,128]{1,0:T(8,128)(2,1)} fusion(f32[256,128]{1,0:T(8,128)} %shard_map.82, bf16[256,128]{1,0:T(8,128)(2,1)S(1)} %copy-done, s32[256,128]{1,0:T(8,128)S(1)} %copy-done.1), kind=kLoop, calls=%fused_computation.1 | loop fusion | flops 196608 | bytes 393216 | tf_op jit(solution)/shard_map/convert_element_type | solution.py:344
Async XLA Ops:
  0.0 14.4 %copy-start = (bf16[256,128]{1,0:T(8,128)(2,1)S(1)}, bf16[256,128]{1,0:T(8,128)(2,1)}, u32[]{:S(2)}) copy-start(bf16[256,128]{1,0:T(8,128)(2,1)} %dwell_hbm.1) | copy-start | bytes 196612
  0.0 14.4 %copy-start.1 = (s32[256,128]{1,0:T(8,128)S(1)}, s32[256,128]{1,0:T(8,128)}, u32[]{:S(2)}) copy-start(s32[256,128]{1,0:T(8,128)} %param.10) | copy-start | bytes 393220

commit v3 on v2

v3 whole, which is shorter than its diff:
```python
import functools

import jax
import jax.numpy as jnp
from jax import lax
from jax.experimental import pallas as pl
from jax.experimental.pallas import tpu as pltpu
from jax.sharding import PartitionSpec as P

MESH = pl.DeviceIdType.MESH
F32 = jnp.float32
BF16 = jnp.bfloat16

TAPS = 63
RADIUS = 31
ROWS = 256
COLS = 128
RIM = 64
RING = 256
OUT = 320
NRATE = 4
SCEN = 16
STEP_SIZE = 1.0


def lanes(shape):
    return lax.broadcasted_iota(jnp.int32, shape, len(shape) - 1)


def kernel(
    n_space,
    n_scen,
    dwell_hbm,
    target_hbm,
    off_hbm,
    level_hbm,
    rate_hbm,
    row_hbm,
    col_hbm,
    bound_hbm,
    next_ref,
    bound_v,
    off_s,
    level_s,
    rate_s,
    off_v,
    level_v,
    row_taps,
    col_taps,
    dwell_x,
    recv_l,
    recv_r,
    corners,
    t_own,
    t_top,
    t_bot,
    wide,
    taps8,
    row_fwd,
    col_mat,
    row_adj,
    col_tall,
    row_tall,
    col_pair,
    t_back,
    t_grad,
    count,
    along,
    back,
    send_sem,
    recv_sem,
    load_sem,
):
    sp = lax.axis_index("space")
    sc = lax.axis_index("scen")
    up, down, left, right = sp - 1, sp + 1, sc - 1, sc + 1
    has_up, has_down = sp > 0, sp < n_space - 1
    has_left, has_right = sc > 0, sc < n_scen - 1
    core = sp % 2
    other = (sc + n_scen // 2) % n_scen
    up_sc = jnp.where(core == 0, other, sc)
    down_sc = jnp.where(core == 0, sc, other)

    def first_tile(c):
        return jnp.minimum(jnp.maximum(c - 1, 0), n_scen - 3)

    def window(c):
        return pl.ds(pl.multiple_of(first_tile(c) * COLS, COLS), 3 * COLS)

    peers = (
        (up, sc, has_up),
        (down, sc, has_down),
        (sp, left, has_left),
        (sp, right, has_right),
        (up, left, has_up & has_left),
        (up, right, has_up & has_right),
        (down, left, has_down & has_left),
        (down, right, has_down & has_right),
        (up, up_sc, has_up),
        (down, down_sc, has_down),
    )
    comes = [peers[k][2] for k in (1, 0, 3, 2, 7, 6, 5, 4, 9, 8)]
    barrier = pltpu.get_barrier_semaphore()
    for row, col, there in [peers[k] for k in (4, 5, 6, 7, 0, 1, 8, 9, 2, 3)]:

        @pl.when(there)
        def _(row=row, col=col):
            pl.semaphore_signal(barrier, inc=1, device_id=(row, col), device_id_type=MESH)

    greeted = sum(jnp.where(there, 1, 0) for _, _, there in peers)

    load_dwell = pltpu.make_async_copy(
        dwell_hbm, dwell_x.at[RIM : RIM + ROWS, 0:COLS], load_sem.at[0]
    )
    load_target = pltpu.make_async_copy(target_hbm.at[:, window(sc)], t_own, load_sem.at[1])
    load_dwell.start()
    load_bound = pltpu.make_async_copy(bound_hbm, bound_v, load_sem.at[9])
    load_bound.start()
    small = [
        pltpu.make_async_copy(src, dst, load_sem.at[2 + k])
        for k, (src, dst) in enumerate(
            (
                (row_hbm, row_taps),
                (col_hbm, col_taps),
                (rate_hbm, rate_s),
                (off_hbm, off_v),
                (level_hbm, level_v),
                (off_hbm, off_s),
                (level_hbm, level_s),
            )
        )
    ]
    for load in small:
        load.start()
    load_target.start()
    load_dwell.wait()
    pl.semaphore_wait(barrier, greeted)

    first_rows, last_rows = slice(0, RIM), slice(ROWS - RIM, ROWS)
    own_tile = dwell_x.at[RIM : RIM + ROWS, 0:COLS]
    own_first, own_last = dwell_x.at[RIM : 2 * RIM, 0:COLS], dwell_x.at[ROWS : ROWS + RIM, 0:COLS]
    pairs = (
        (own_first, dwell_x.at[RIM + ROWS : RIM + ROWS + RIM, 0:COLS]),
        (own_last, dwell_x.at[0:RIM, 0:COLS]),
        (own_tile, recv_r),
        (own_tile, recv_l),
        (own_first, corners.at[3]),
        (own_first, corners.at[2]),
        (own_last, corners.at[1]),
        (own_last, corners.at[0]),
        (target_hbm.at[first_rows, window(up_sc)], t_bot),
        (target_hbm.at[last_rows, window(down_sc)], t_top),
    )
    copies = [
        pltpu.make_async_remote_copy(
            src_ref=src,
            dst_ref=dst,
            send_sem=send_sem.at[k],
            recv_sem=recv_sem.at[k],
            device_id=peers[k][:2],
            device_id_type=MESH,
        )
        for k, (src, dst) in enumerate(pairs)
    ]
    for k in (4, 5, 6, 7, 8, 9, 0, 1, 2, 3):
        pl.when(peers[k][2])(copies[k].start)

    def arrive(ks):
        for k in ks:
            pl.when(comes[k])(copies[k].wait_recv)

    side_ok = jnp.where(lanes((1, COLS)) < RIM, jnp.where(has_right, 1, 0), jnp.where(has_left, 1, 0)) > 0
    low = lanes((1, COLS)) < RIM

    for load in small:
        load.wait()

    taps8[...] = jnp.zeros_like(taps8)
    taps8[0:NRATE, 0:TAPS] = row_taps[...].astype(F32)
    taps8[4 : 4 + NRATE, 0:TAPS] = col_taps[...].astype(F32)
    taps = taps8[...]
    flip = jnp.where(
        lax.broadcasted_iota(jnp.int32, (RING, RING), 0) + lanes((RING, RING)) == TAPS - 1, 1.0, 0.0
    ).astype(BF16)
    reversed_taps = jnp.dot(taps.astype(BF16), flip, preferred_element_type=F32)

    def toeplitz(line, count_, first):
        return pltpu.roll(
            jnp.broadcast_to(line, (count_, RING)), first % RING, 1, stride=1, stride_axis=0
        )

    for q in range(NRATE):
        band = toeplitz(taps[q : q + 1], 192, 1).astype(BF16)
        row_fwd[0, 160 * q : 160 * q + 160, :] = band[0:160]
        row_fwd[1, 160 * q : 160 * q + 160, :] = band[32:192]
        band = toeplitz(taps[4 + q : 5 + q], 320, -RADIUS - 32)
        col_tall[q] = band[:, 0:COLS]
        col_mat[q] = band[32 : 32 + RING].astype(BF16)
        band = toeplitz(reversed_taps[q : q + 1], 192, 1)
        row_tall[q, 0] = band[:, 0:COLS]
        row_tall[q, 1] = band[:, COLS:RING]
        row_adj[:, RING * q : RING * q + RING] = band[0:128].astype(BF16)

    offs = off_v[...]
    row_at = sp * ROWS + lax.broadcasted_iota(jnp.int32, (OUT, SCEN), 0) - 32 + offs[0:1, :]
    row_in = jnp.where((row_at >= 0) & (row_at < n_space * ROWS), 1.0, 0.0).astype(BF16)
    ring_at = lax.broadcasted_iota(jnp.int32, (RING, SCEN), 0)
    col_at = jnp.where(ring_at < COLS + RIM, ring_at, ring_at - RING) + sc * COLS + offs[1:2, :]
    col_in = jnp.where((col_at >= 0) & (col_at < n_scen * COLS), 1.0, 0.0)
    levels = level_v[...]
    for q in range(NRATE):
        mine = jnp.where(levels == q, 1.0, 0.0)
        seen = lax.dot_general(
            row_in, (col_in * mine).astype(BF16), (((1,), (1,)), ((), ())), preferred_element_type=F32
        )
        rate = rate_s[q]
        count[q] = seen * (rate * rate * (1.0 / SCEN))

    at = sc - first_tile(sc)

    def to_ring(ref):
        own = ref[:, pl.ds(pl.multiple_of(at * COLS, COLS), COLS)].astype(F32)
        after = ref[:, pl.ds(pl.multiple_of(jnp.minimum(at + 1, 2) * COLS, COLS), COLS)].astype(F32)
        before = ref[:, pl.ds(pl.multiple_of(jnp.maximum(at - 1, 0) * COLS, COLS), COLS)].astype(F32)
        return own, jnp.where(side_ok, jnp.where(low, after, before), 0.0)

    load_target.wait()
    own, side = to_ring(t_own)
    wide[RIM : RIM + ROWS, 0:COLS] = own.astype(BF16)
    wide[RIM : RIM + ROWS, COLS:RING] = side.astype(BF16)

    shift_rows = [off_s[0, s] for s in range(SCEN)]
    shift_cols = [off_s[1, s] for s in range(SCEN)]
    level_of = [level_s[0, s] for s in range(SCEN)]
    weights = [rate_s[level_of[s]] * (1.0 / SCEN) for s in range(SCEN)]

    for pair in range(SCEN // 2):
        bands = [
            col_tall[level_of[s], pl.ds(32 - shift_cols[s], RING), :].astype(BF16)
            for s in (2 * pair, 2 * pair + 1)
        ]
        both = jnp.concatenate(bands, axis=1)
        col_pair[pair] = both
        product = jnp.dot(wide[RIM : RIM + ROWS, :], both, preferred_element_type=F32)
        for k in range(2):
            s = 2 * pair + k
            part = (product[:, COLS * k : COLS * k + COLS] * weights[s]).astype(BF16)
            t_back[s, RIM:256, 0:COLS] = part[0:192]
            t_back[s, 0:192, COLS:RING] = part[64:256]

    arrive((8, 9))
    for ref, there, begin in ((t_top, has_up, 0), (t_bot, has_down, RIM + ROWS)):
        own, side = to_ring(ref)
        wide[begin : begin + RIM, 0:COLS] = jnp.where(there, own, 0.0).astype(BF16)
        wide[begin : begin + RIM, COLS:RING] = jnp.where(there, side, 0.0).astype(BF16)
    rims = jnp.concatenate([wide[0:RIM, :], wide[RIM + ROWS :, :]], axis=0)
    for pair in range(SCEN // 2):
        product = jnp.dot(rims, col_pair[pair], preferred_element_type=F32)
        for k in range(2):
            s = 2 * pair + k
            part = (product[:, COLS * k : COLS * k + COLS] * weights[s]).astype(BF16)
            t_back[s, 0:RIM, 0:COLS] = part[0:RIM]
            t_back[s, 192:256, COLS:RING] = part[RIM:]
    total = jnp.zeros((128, RING), F32)
    for s in range(SCEN):
        band = jnp.concatenate(
            [row_tall[level_of[s], half, pl.ds(32 + shift_rows[s], 128), :] for half in range(2)], axis=1
        ).astype(BF16)
        total = total + jnp.dot(band, t_back[s], preferred_element_type=F32)
    t_grad[...] = total

    arrive(range(8))

    def corner(before, after, there):
        x = jnp.where(low, corners[after].astype(F32), corners[before].astype(F32))
        return jnp.where(there, jnp.where(side_ok, x, 0.0), 0.0).astype(BF16)

    dwell_x[0:RIM, 0:COLS] = jnp.where(has_up, dwell_x[0:RIM, 0:COLS].astype(F32), 0.0).astype(BF16)
    dwell_x[RIM + ROWS :, 0:COLS] = jnp.where(has_down, dwell_x[RIM + ROWS :, 0:COLS].astype(F32), 0.0).astype(BF16)
    dwell_x[0:RIM, COLS:RING] = corner(0, 1, has_up)
    dwell_x[RIM + ROWS :, COLS:RING] = corner(2, 3, has_down)
    dwell_x[RIM : RIM + ROWS, COLS:RING] = jnp.where(
        side_ok, jnp.where(low, recv_r[...].astype(F32), recv_l[...].astype(F32)), 0.0
    ).astype(BF16)

    for half in range(2):
        product = jnp.dot(
            row_fwd[half], dwell_x[128 * half : 128 * half + 256, :], preferred_element_type=F32
        ).astype(BF16)
        for q in range(NRATE):
            along[q, 160 * half : 160 * half + 160, :] = product[160 * q : 160 * q + 160]

    for q in range(NRATE):
        base = lax.dot_general(
            along[q], col_mat[q], (((1,), (1,)), ((), ())), preferred_element_type=F32
        )
        misfit = (count[q] * base).astype(BF16)
        product = jnp.dot(misfit, col_mat[q, :, 0:COLS], preferred_element_type=F32).astype(BF16)
        back[RING * q : RING * q + 256, 0:COLS] = product[0:256]
        back[RING * q : RING * q + 192, COLS:RING] = product[128:OUT]
        back[RING * q + 192 : RING * q + 256, COLS:RING] = jnp.zeros((64, COLS), BF16)

    grad = jnp.dot(row_adj[...], back[...], preferred_element_type=F32) - t_grad[...]
    load_bound.wait()
    for half in range(2):
        rows = slice(128 * half, 128 * half + 128)
        dwell = dwell_x[RIM + 128 * half : RIM + 128 * half + 128, 0:COLS].astype(F32)
        stepped = dwell - STEP_SIZE * grad[:, COLS * half : COLS * half + COLS]
        kept = jnp.where(bound_v[rows, :] == 1, jnp.maximum(stepped, 0.0), stepped)
        next_ref[rows, :] = kept.astype(BF16)
    for k in range(10):
        pl.when(peers[k][2])(copies[k].wait_send)


def tile_step(n_space, n_scen, dwell, target, bound, offsets, level, rates, row_kernels, col_kernels):
    offsets, level = offsets.T, level.T
    vmem = pl.BlockSpec(memory_space=pltpu.VMEM)
    far = pl.BlockSpec(memory_space=pltpu.HBM)
    return pl.pallas_call(
        functools.partial(kernel, n_space, n_scen),
        out_shape=pltpu.VMEM((ROWS, COLS), BF16),
        in_specs=[far] * 8,
        out_specs=vmem,
        scratch_shapes=[
            pltpu.VMEM((ROWS, COLS), jnp.int32),
            pltpu.SMEM((2, SCEN), jnp.int32),
            pltpu.SMEM((1, SCEN), jnp.int32),
            pltpu.SMEM((NRATE,), F32),
            pltpu.VMEM((2, SCEN), jnp.int32),
            pltpu.VMEM((1, SCEN), jnp.int32),
            pltpu.VMEM((NRATE, TAPS), BF16),
            pltpu.VMEM((NRATE, TAPS), BF16),
            pltpu.VMEM((384, RING), BF16),
            pltpu.VMEM((ROWS, COLS), BF16),
            pltpu.VMEM((ROWS, COLS), BF16),
            pltpu.VMEM((4, RIM, COLS), BF16),
            pltpu.VMEM((ROWS, 3 * COLS), BF16),
            pltpu.VMEM((RIM, 3 * COLS), BF16),
            pltpu.VMEM((RIM, 3 * COLS), BF16),
            pltpu.VMEM((384, RING), BF16),
            pltpu.VMEM((8, RING), F32),
            pltpu.VMEM((2, NRATE * 160, RING), BF16),
            pltpu.VMEM((NRATE, RING, RING), BF16),
            pltpu.VMEM((128, NRATE * RING), BF16),
            pltpu.VMEM((NRATE, OUT, COLS), F32),
            pltpu.VMEM((NRATE, 2, 192, COLS), F32),
            pltpu.VMEM((SCEN // 2, RING, RING), BF16),
            pltpu.VMEM((SCEN, RING, RING), BF16),
            pltpu.VMEM((128, RING), F32),
            pltpu.VMEM((NRATE, OUT, RING), F32),
            pltpu.VMEM((NRATE, OUT, RING), BF16),
            pltpu.VMEM((NRATE * RING, RING), BF16),
            pltpu.SemaphoreType.DMA((10,)),
            pltpu.SemaphoreType.DMA((10,)),
            pltpu.SemaphoreType.DMA((10,)),
        ],
        compiler_params=pltpu.CompilerParams(collective_id=0, vmem_limit_bytes=48 * 1024 * 1024),
    )(*(pltpu.with_memory_space_constraint(x, pltpu.HBM) for x in (dwell, target, offsets, level, rates, row_kernels, col_kernels, bound)))


def solution(mesh):
    return jax.shard_map(
        functools.partial(tile_step, mesh.shape["space"], mesh.shape["scen"]),
        mesh=mesh,
        in_specs=(P("space", "scen"), P("space", None), P("space", "scen"), P(), P(), P(), P(), P()),
        out_specs=P("space", "scen"),
        check_vma=False,
    )
```

time: 16.1 us -> 13.7 us (0.85)
  other arithmetic: 1.56 us -> 0 us
  Pallas kernels: 14.3 us -> 13 us
  local copies, waits for them, and re-layouts: 0.01 us -> 0.63 us
    convert_element_type x1 -> x0, other arithmetic: 1.56 us -> none  [tile_step(): jnp.where(bound == 1, jnp.maximum(stepped, 0.0), stepped).astype(BF16)]
    pallas_call x1, Pallas kernels: 14.3 us -> 13 us  [tile_step(): pl.pallas_call(functools.partial(kernel, n_space, n_scen), out_shape=pltp...]
    unnamed x4 -> x1, local copies, waits for them, and re-layouts: 0.01 us -> 0.63 us
where the time goes in v3:
time: 13.7 us; the launch traced here: 13.6 us
  Pallas kernels  13 us (95%)
  local copies, waits for them, and re-layouts  0.63 us (5%)
    pallas_call x1, Pallas kernels, tile_step(): pl.pallas_call(functools.partial(kernel, n_space, n_scen), out_shape=pltp...  13 us
    unnamed x1, local copies, waits for them, and re-layouts  0.63 us

profile of v3, /device:TPU:1, one launch (start us, length us, event | category | flops | bytes accessed | tf_op | source)
XLA Modules:
  0.0 13.6 jit_solution(9033228661690925035)
XLA Ops:
  0.0 13.0 %shard_map.82 = bf16[256,128]{1,0:T(8,128)(2,1)S(1)} custom-call(bf16[256,128]{1,0:T(8,128)(2,1)} %dwell_hbm.1, bf16[256,1024]{1,0:T(8,128)(2,1)} %target_hbm.1, s32[2,16]{1,0:T(2,128)} %bitcast.2, s32[1,16]{1,0:T(1,128)} %bitcast.3, f32[4]{0:T(128)} %rate_hbm.1, bf16[4,63]{1,0:T(4,128)(2,1)} %row_hbm.1, bf16[4,63]{1,0:T(4,128)(2,1)} %col_hbm.1, ...), custom_call_target="tpu_custom_call" | custom-call | tf_op jit(solution)/shard_map/pallas_call | solution.py:319
  13.0 0.6 %copy.10 = bf16[256,128]{1,0:T(8,128)(2,1)} copy(bf16[256,128]{1,0:T(8,128)(2,1)S(1)} %shard_map.82) | data formatting | bytes 131072

commit v4 on v3

--- a/solution.py
+++ b/solution.py
@@ -48,6 +48,11 @@
     row_taps,
     col_taps,
     dwell_x,
+    tile,
+    rim_up,
+    rim_down,
+    pack_l,
+    pack_r,
     recv_l,
     recv_r,
     corners,
@@ -65,6 +70,7 @@
     t_back,
     t_grad,
     count,
+    rim_band,
     along,
     back,
     send_sem,
@@ -110,7 +116,7 @@
     greeted = sum(jnp.where(there, 1, 0) for _, _, there in peers)
 
     load_dwell = pltpu.make_async_copy(
-        dwell_hbm, dwell_x.at[RIM : RIM + ROWS, 0:COLS], load_sem.at[0]
+        dwell_hbm, tile, load_sem.at[0]
     )
     load_target = pltpu.make_async_copy(target_hbm.at[:, window(sc)], t_own, load_sem.at[1])
     load_dwell.start()
@@ -134,16 +140,20 @@
         load.start()
     load_target.start()
     load_dwell.wait()
+    low = lanes((1, COLS)) < RIM
+    upper = tile[0:128, :].astype(F32)
+    lower = pltpu.roll(tile[128:256, :].astype(F32), RIM, 1)
+    pack_l[...] = jnp.where(low, upper, lower).astype(BF16)
+    pack_r[...] = jnp.where(low, lower, upper).astype(BF16)
     pl.semaphore_wait(barrier, greeted)
 
     first_rows, last_rows = slice(0, RIM), slice(ROWS - RIM, ROWS)
-    own_tile = dwell_x.at[RIM : RIM + ROWS, 0:COLS]
-    own_first, own_last = dwell_x.at[RIM : 2 * RIM, 0:COLS], dwell_x.at[ROWS : ROWS + RIM, 0:COLS]
+    own_first, own_last = tile.at[first_rows], tile.at[last_rows]
     pairs = (
-        (own_first, dwell_x.at[RIM + ROWS : RIM + ROWS + RIM, 0:COLS]),
-        (own_last, dwell_x.at[0:RIM, 0:COLS]),
-        (own_tile, recv_r),
-        (own_tile, recv_l),
+        (own_first, rim_down),
+        (own_last, rim_up),
+        (pack_l, recv_r),
+        (pack_r, recv_l),
         (own_first, corners.at[3]),
         (own_first, corners.at[2]),
         (own_last, corners.at[1]),
@@ -247,27 +257,34 @@
             part = (product[:, COLS * k : COLS * k + COLS] * weights[s]).astype(BF16)
             t_back[s, RIM:256, 0:COLS] = part[0:192]
             t_back[s, 0:192, COLS:RING] = part[64:256]
-
+            t_back[s, 0:RIM, 0:COLS] = jnp.zeros((RIM, COLS), BF16)
+            t_back[s, 192:256, COLS:RING] = jnp.zeros((RIM, COLS), BF16)
+            first = row_tall[level_of[s], 0, pl.ds(32 + shift_rows[s], 128), :]
+            second = row_tall[level_of[s], 1, pl.ds(32 + shift_rows[s], 128), :]
+            term = jnp.dot(
+                jnp.concatenate([first, second], axis=1).astype(BF16), t_back[s], preferred_element_type=F32
+            )
+            t_grad[...] = term if s == 0 else t_grad[...] + term
+            lanes_ = slice(COLS * k, COLS * k + COLS)
+            rim_band[pair, 0:64, lanes_] = jnp.where(low, first[0:64], 0.0).astype(BF16)
+            rim_band[pair, 64:128, lanes_] = jnp.where(low, 0.0, second[64:128]).astype(BF16)
+
+    dwell_x[RIM : RIM + ROWS, 0:COLS] = tile[...]
     arrive((8, 9))
     for ref, there, begin in ((t_top, has_up, 0), (t_bot, has_down, RIM + ROWS)):
         own, side = to_ring(ref)
         wide[begin : begin + RIM, 0:COLS] = jnp.where(there, own, 0.0).astype(BF16)
         wide[begin : begin + RIM, COLS:RING] = jnp.where(there, side, 0.0).astype(BF16)
     rims = jnp.concatenate([wide[0:RIM, :], wide[RIM + ROWS :, :]], axis=0)
+    total = jnp.zeros((128, COLS), F32)
     for pair in range(SCEN // 2):
         product = jnp.dot(rims, col_pair[pair], preferred_element_type=F32)
-        for k in range(2):
-            s = 2 * pair + k
-            part = (product[:, COLS * k : COLS * k + COLS] * weights[s]).astype(BF16)
-            t_back[s, 0:RIM, 0:COLS] = part[0:RIM]
-            t_back[s, 192:256, COLS:RING] = part[RIM:]
-    total = jnp.zeros((128, RING), F32)
-    for s in range(SCEN):
-        band = jnp.concatenate(
-            [row_tall[level_of[s], half, pl.ds(32 + shift_rows[s], 128), :] for half in range(2)], axis=1
-        ).astype(BF16)
-        total = total + jnp.dot(band, t_back[s], preferred_element_type=F32)
-    t_grad[...] = total
+        parts = [
+            (product[:, COLS * k : COLS * k + COLS] * weights[2 * pair + k]).astype(BF16) for k in range(2)
+        ]
+        total = total + jnp.dot(rim_band[pair], jnp.concatenate(parts, axis=0), preferred_element_type=F32)
+    t_grad[0:64, 0:COLS] += total[0:64]
+    t_grad[64:128, COLS:RING] += total[64:128]
 
     arrive(range(8))
 
@@ -275,13 +292,15 @@
         x = jnp.where(low, corners[after].astype(F32), corners[before].astype(F32))
         return jnp.where(there, jnp.where(side_ok, x, 0.0), 0.0).astype(BF16)
 
-    dwell_x[0:RIM, 0:COLS] = jnp.where(has_up, dwell_x[0:RIM, 0:COLS].astype(F32), 0.0).astype(BF16)
-    dwell_x[RIM + ROWS :, 0:COLS] = jnp.where(has_down, dwell_x[RIM + ROWS :, 0:COLS].astype(F32), 0.0).astype(BF16)
+    dwell_x[0:RIM, 0:COLS] = jnp.where(has_up, rim_up[...].astype(F32), 0.0).astype(BF16)
+    dwell_x[RIM + ROWS :, 0:COLS] = jnp.where(has_down, rim_down[...].astype(F32), 0.0).astype(BF16)
     dwell_x[0:RIM, COLS:RING] = corner(0, 1, has_up)
     dwell_x[RIM + ROWS :, COLS:RING] = corner(2, 3, has_down)
-    dwell_x[RIM : RIM + ROWS, COLS:RING] = jnp.where(
-        side_ok, jnp.where(low, recv_r[...].astype(F32), recv_l[...].astype(F32)), 0.0
-    ).astype(BF16)
+    after, before = recv_r[...].astype(F32), recv_l[...].astype(F32)
+    upper = jnp.where(low, after, before)
+    lower = pltpu.roll(jnp.where(low, before, after), RIM, 1)
+    dwell_x[RIM : RIM + 128, COLS:RING] = jnp.where(side_ok, upper, 0.0).astype(BF16)
+    dwell_x[RIM + 128 : RIM + ROWS, COLS:RING] = jnp.where(side_ok, lower, 0.0).astype(BF16)
 
     for half in range(2):
         product = jnp.dot(
@@ -332,7 +351,12 @@
             pltpu.VMEM((NRATE, TAPS), BF16),
             pltpu.VMEM((384, RING), BF16),
             pltpu.VMEM((ROWS, COLS), BF16),
-            pltpu.VMEM((ROWS, COLS), BF16),
+            pltpu.VMEM((RIM, COLS), BF16),
+            pltpu.VMEM((RIM, COLS), BF16),
+            pltpu.VMEM((128, COLS), BF16),
+            pltpu.VMEM((128, COLS), BF16),
+            pltpu.VMEM((128, COLS), BF16),
+            pltpu.VMEM((128, COLS), BF16),
             pltpu.VMEM((4, RIM, COLS), BF16),
             pltpu.VMEM((ROWS, 3 * COLS), BF16),
             pltpu.VMEM((RIM, 3 * COLS), BF16),
@@ -348,6 +372,7 @@
             pltpu.VMEM((SCEN, RING, RING), BF16),
             pltpu.VMEM((128, RING), F32),
             pltpu.VMEM((NRATE, OUT, RING), F32),
+            pltpu.VMEM((SCEN // 2, 128, RING), BF16),
             pltpu.VMEM((NRATE, OUT, RING), BF16),
             pltpu.VMEM((NRATE * RING, RING), BF16),
             pltpu.SemaphoreType.DMA((10,)),

time: 13.7 us -> 13.2 us (0.964)
  the two profiles are of different devices: /device:TPU:1 before, /device:TPU:256 now
where the time goes in v4:
time: 13.2 us; the launch traced here: 13.1 us
  Pallas kernels  12.5 us (95%)
  local copies, waits for them, and re-layouts  0.63 us (5%)
    pallas_call x1, Pallas kernels, tile_step(): pl.pallas_call(functools.partial(kernel, n_space, n_scen), out_shape=pltp...  12.5 us
    unnamed x1, local copies, waits for them, and re-layouts  0.63 us

profile of v4, /device:TPU:256, one launch (start us, length us, event | category | flops | bytes accessed | tf_op | source)
XLA Modules:
  0.0 13.1 jit_solution(13161581542446140628)
XLA Ops:
  0.0 12.5 %shard_map.82 = bf16[256,128]{1,0:T(8,128)(2,1)S(1)} custom-call(bf16[256,128]{1,0:T(8,128)(2,1)} %dwell_hbm.1, bf16[256,1024]{1,0:T(8,128)(2,1)} %target_hbm.1, s32[2,16]{1,0:T(2,128)} %bitcast.2, s32[1,16]{1,0:T(1,128)} %bitcast.3, f32[4]{0:T(128)} %rate_hbm.1, bf16[4,63]{1,0:T(4,128)(2,1)} %row_hbm.1, bf16[4,63]{1,0:T(4,128)(2,1)} %col_hbm.1, ...), custom_call_target="tpu_custom_call" | custom-call | tf_op jit(solution)/shard_map/pallas_call | solution.py:338
  12.5 0.6 %copy.10 = bf16[256,128]{1,0:T(8,128)(2,1)} copy(bf16[256,128]{1,0:T(8,128)(2,1)S(1)} %shard_map.82) | data formatting | bytes 131072

commit v5 on v4

--- a/solution.py
+++ b/solution.py
@@ -57,6 +57,8 @@
     recv_r,
     corners,
     t_own,
+    t_raw,
+    t_send,
     t_top,
     t_bot,
     wide,
@@ -119,7 +121,15 @@
         dwell_hbm, tile, load_sem.at[0]
     )
     load_target = pltpu.make_async_copy(target_hbm.at[:, window(sc)], t_own, load_sem.at[1])
+    load_rims = [
+        pltpu.make_async_copy(
+            target_hbm.at[slice(begin, begin + RIM), window(col)], t_raw.at[k], load_sem.at[10 + k]
+        )
+        for k, (begin, col) in enumerate(((0, up_sc), (ROWS - RIM, down_sc)))
+    ]
     load_dwell.start()
+    for load in load_rims:
+        load.start()
     load_bound = pltpu.make_async_copy(bound_hbm, bound_v, load_sem.at[9])
     load_bound.start()
     small = [
@@ -141,10 +151,37 @@
     load_target.start()
     load_dwell.wait()
     low = lanes((1, COLS)) < RIM
+
+    def to_ring(ref, col):
+        at = col - first_tile(col)
+
+        def pick(k):
+            return ref[:, pl.ds(pl.multiple_of(k * COLS, COLS), COLS)].astype(F32)
+
+        after = jnp.where(col < n_scen - 1, pick(jnp.minimum(at + 1, 2)), 0.0)
+        before = jnp.where(col > 0, pick(jnp.maximum(at - 1, 0)), 0.0)
+        return pick(at), jnp.where(low, after, before)
+
     upper = tile[0:128, :].astype(F32)
     lower = pltpu.roll(tile[128:256, :].astype(F32), RIM, 1)
     pack_l[...] = jnp.where(low, upper, lower).astype(BF16)
     pack_r[...] = jnp.where(low, lower, upper).astype(BF16)
+    for k, col in enumerate((up_sc, down_sc)):
+        load_rims[k].wait()
+        own, side = to_ring(t_raw.at[k], col)
+        t_send[k, :, 0:COLS] = own.astype(BF16)
+        t_send[k, :, COLS:RING] = side.astype(BF16)
+
+    @pl.when(sp == 0)
+    def _():
+        t_top[...] = jnp.zeros_like(t_top)
+        rim_up[...] = jnp.zeros_like(rim_up)
+
+    @pl.when(sp == n_space - 1)
+    def _():
+        t_bot[...] = jnp.zeros_like(t_bot)
+        rim_down[...] = jnp.zeros_like(rim_down)
+
     pl.semaphore_wait(barrier, greeted)
 
     first_rows, last_rows = slice(0, RIM), slice(ROWS - RIM, ROWS)
@@ -158,8 +195,8 @@
         (own_first, corners.at[2]),
         (own_last, corners.at[1]),
         (own_last, corners.at[0]),
-        (target_hbm.at[first_rows, window(up_sc)], t_bot),
-        (target_hbm.at[last_rows, window(down_sc)], t_top),
+        (t_send.at[0], t_bot),
+        (t_send.at[1], t_top),
     )
     copies = [
         pltpu.make_async_remote_copy(
@@ -172,7 +209,7 @@
         )
         for k, (src, dst) in enumerate(pairs)
     ]
-    for k in (4, 5, 6, 7, 8, 9, 0, 1, 2, 3):
+    for k in (8, 9, 4, 5, 6, 7, 0, 1, 2, 3):
         pl.when(peers[k][2])(copies[k].start)
 
     def arrive(ks):
@@ -226,18 +263,10 @@
         rate = rate_s[q]
         count[q] = seen * (rate * rate * (1.0 / SCEN))
 
-    at = sc - first_tile(sc)
-
-    def to_ring(ref):
-        own = ref[:, pl.ds(pl.multiple_of(at * COLS, COLS), COLS)].astype(F32)
-        after = ref[:, pl.ds(pl.multiple_of(jnp.minimum(at + 1, 2) * COLS, COLS), COLS)].astype(F32)
-        before = ref[:, pl.ds(pl.multiple_of(jnp.maximum(at - 1, 0) * COLS, COLS), COLS)].astype(F32)
-        return own, jnp.where(side_ok, jnp.where(low, after, before), 0.0)
-
     load_target.wait()
-    own, side = to_ring(t_own)
-    wide[RIM : RIM + ROWS, 0:COLS] = own.astype(BF16)
-    wide[RIM : RIM + ROWS, COLS:RING] = side.astype(BF16)
+    own, side = to_ring(t_own, sc)
+    wide[:, 0:COLS] = own.astype(BF16)
+    wide[:, COLS:RING] = side.astype(BF16)
 
     shift_rows = [off_s[0, s] for s in range(SCEN)]
     shift_cols = [off_s[1, s] for s in range(SCEN)]
@@ -251,7 +280,7 @@
         ]
         both = jnp.concatenate(bands, axis=1)
         col_pair[pair] = both
-        product = jnp.dot(wide[RIM : RIM + ROWS, :], both, preferred_element_type=F32)
+        product = jnp.dot(wide[...], both, preferred_element_type=F32)
         for k in range(2):
             s = 2 * pair + k
             part = (product[:, COLS * k : COLS * k + COLS] * weights[s]).astype(BF16)
@@ -271,11 +300,7 @@
 
     dwell_x[RIM : RIM + ROWS, 0:COLS] = tile[...]
     arrive((8, 9))
-    for ref, there, begin in ((t_top, has_up, 0), (t_bot, has_down, RIM + ROWS)):
-        own, side = to_ring(ref)
-        wide[begin : begin + RIM, 0:COLS] = jnp.where(there, own, 0.0).astype(BF16)
-        wide[begin : begin + RIM, COLS:RING] = jnp.where(there, side, 0.0).astype(BF16)
-    rims = jnp.concatenate([wide[0:RIM, :], wide[RIM + ROWS :, :]], axis=0)
+    rims = jnp.concatenate([t_top[...], t_bot[...]], axis=0)
     total = jnp.zeros((128, COLS), F32)
     for pair in range(SCEN // 2):
         product = jnp.dot(rims, col_pair[pair], preferred_element_type=F32)
@@ -286,21 +311,25 @@
     t_grad[0:64, 0:COLS] += total[0:64]
     t_grad[64:128, COLS:RING] += total[64:128]
 
-    arrive(range(8))
-
-    def corner(before, after, there):
-        x = jnp.where(low, corners[after].astype(F32), corners[before].astype(F32))
-        return jnp.where(there, jnp.where(side_ok, x, 0.0), 0.0).astype(BF16)
-
-    dwell_x[0:RIM, 0:COLS] = jnp.where(has_up, rim_up[...].astype(F32), 0.0).astype(BF16)
-    dwell_x[RIM + ROWS :, 0:COLS] = jnp.where(has_down, rim_down[...].astype(F32), 0.0).astype(BF16)
-    dwell_x[0:RIM, COLS:RING] = corner(0, 1, has_up)
-    dwell_x[RIM + ROWS :, COLS:RING] = corner(2, 3, has_down)
+    arrive((2, 3))
     after, before = recv_r[...].astype(F32), recv_l[...].astype(F32)
     upper = jnp.where(low, after, before)
     lower = pltpu.roll(jnp.where(low, before, after), RIM, 1)
     dwell_x[RIM : RIM + 128, COLS:RING] = jnp.where(side_ok, upper, 0.0).astype(BF16)
     dwell_x[RIM + 128 : RIM + ROWS, COLS:RING] = jnp.where(side_ok, lower, 0.0).astype(BF16)
+
+    arrive((0, 1))
+    dwell_x[0:RIM, 0:COLS] = rim_up[...]
+    dwell_x[RIM + ROWS :, 0:COLS] = rim_down[...]
+
+    arrive((4, 5, 6, 7))
+
+    def corner(before, after, there):
+        x = jnp.where(low, corners[after].astype(F32), corners[before].astype(F32))
+        return jnp.where(there, jnp.where(side_ok, x, 0.0), 0.0).astype(BF16)
+
+    dwell_x[0:RIM, COLS:RING] = corner(0, 1, has_up)
+    dwell_x[RIM + ROWS :, COLS:RING] = corner(2, 3, has_down)
 
     for half in range(2):
         product = jnp.dot(
@@ -359,9 +388,11 @@
             pltpu.VMEM((128, COLS), BF16),
             pltpu.VMEM((4, RIM, COLS), BF16),
             pltpu.VMEM((ROWS, 3 * COLS), BF16),
-            pltpu.VMEM((RIM, 3 * COLS), BF16),
-            pltpu.VMEM((RIM, 3 * COLS), BF16),
-            pltpu.VMEM((384, RING), BF16),
+            pltpu.VMEM((2, RIM, 3 * COLS), BF16),
+            pltpu.VMEM((2, RIM, RING), BF16),
+            pltpu.VMEM((RIM, RING), BF16),
+            pltpu.VMEM((RIM, RING), BF16),
+            pltpu.VMEM((ROWS, RING), BF16),
             pltpu.VMEM((8, RING), F32),
             pltpu.VMEM((2, NRATE * 160, RING), BF16),
             pltpu.VMEM((NRATE, RING, RING), BF16),
@@ -377,7 +408,7 @@
             pltpu.VMEM((NRATE * RING, RING), BF16),
             pltpu.SemaphoreType.DMA((10,)),
             pltpu.SemaphoreType.DMA((10,)),
-            pltpu.SemaphoreType.DMA((10,)),
+            pltpu.SemaphoreType.DMA((12,)),
         ],
         compiler_params=pltpu.CompilerParams(collective_id=0, vmem_limit_bytes=48 * 1024 * 1024),
     )(*(pltpu.with_memory_space_constraint(x, pltpu.HBM) for x in (dwell, target, offsets, level, rates, row_kernels, col_kernels, bound)))

time: 13.2 us -> 12.9 us (0.977)
  the two profiles are of different devices: /device:TPU:256 before, /device:TPU:1 now
where the time goes in v5:
time: 12.9 us; the launch traced here: 12.7 us
  Pallas kernels  12.1 us (94%)
  local copies, waits for them, and re-layouts  0.63 us (5%)
    pallas_call x1, Pallas kernels, tile_step(): pl.pallas_call(functools.partial(kernel, n_space, n_scen), out_shape=pltp...  12.1 us
    unnamed x1, local copies, waits for them, and re-layouts  0.63 us

profile of v5, /device:TPU:1, one launch (start us, length us, event | category | flops | bytes accessed | tf_op | source)
XLA Modules:
  0.0 12.7 jit_solution(3505480601535860311)
XLA Ops:
  0.0 12.1 %shard_map.82 = bf16[256,128]{1,0:T(8,128)(2,1)S(1)} custom-call(bf16[256,128]{1,0:T(8,128)(2,1)} %dwell_hbm.1, bf16[256,1024]{1,0:T(8,128)(2,1)} %target_hbm.1, s32[2,16]{1,0:T(2,128)} %bitcast.2, s32[1,16]{1,0:T(1,128)} %bitcast.3, f32[4]{0:T(128)} %rate_hbm.1, bf16[4,63]{1,0:T(4,128)(2,1)} %row_hbm.1, bf16[4,63]{1,0:T(4,128)(2,1)} %col_hbm.1, ...), custom_call_target="tpu_custom_call" | custom-call | tf_op jit(solution)/shard_map/pallas_call | solution.py:367
  12.1 0.6 %copy.10 = bf16[256,128]{1,0:T(8,128)(2,1)} copy(bf16[256,128]{1,0:T(8,128)(2,1)S(1)} %shard_map.82) | data formatting | bytes 131072

commit v6 on v5

--- a/solution.py
+++ b/solution.py
@@ -162,10 +162,11 @@
         before = jnp.where(col > 0, pick(jnp.maximum(at - 1, 0)), 0.0)
         return pick(at), jnp.where(low, after, before)
 
-    upper = tile[0:128, :].astype(F32)
-    lower = pltpu.roll(tile[128:256, :].astype(F32), RIM, 1)
-    pack_l[...] = jnp.where(low, upper, lower).astype(BF16)
-    pack_r[...] = jnp.where(low, lower, upper).astype(BF16)
+    for g in range(4):
+        upper = tile[64 * g : 64 * g + 32, :].astype(F32)
+        lower = pltpu.roll(tile[64 * g + 32 : 64 * g + 64, :].astype(F32), RIM, 1)
+        pack_l[32 * g : 32 * g + 32, :] = jnp.where(low, upper, lower).astype(BF16)
+        pack_r[32 * g : 32 * g + 32, :] = jnp.where(low, lower, upper).astype(BF16)
     for k, col in enumerate((up_sc, down_sc)):
         load_rims[k].wait()
         own, side = to_ring(t_raw.at[k], col)
@@ -191,10 +192,10 @@
         (own_last, rim_up),
         (pack_l, recv_r),
         (pack_r, recv_l),
-        (own_first, corners.at[3]),
-        (own_first, corners.at[2]),
-        (own_last, corners.at[1]),
-        (own_last, corners.at[0]),
+        (pack_l.at[0:32], corners.at[3]),
+        (pack_r.at[0:32], corners.at[2]),
+        (pack_l.at[96:128], corners.at[1]),
+        (pack_r.at[96:128], corners.at[0]),
         (t_send.at[0], t_bot),
         (t_send.at[1], t_top),
     )
@@ -209,7 +210,7 @@
         )
         for k, (src, dst) in enumerate(pairs)
     ]
-    for k in (8, 9, 4, 5, 6, 7, 0, 1, 2, 3):
+    for k in (8, 9, 4, 5, 6, 7, 2, 3, 0, 1):
         pl.when(peers[k][2])(copies[k].start)
 
     def arrive(ks):
@@ -312,11 +313,17 @@
     t_grad[64:128, COLS:RING] += total[64:128]
 
     arrive((2, 3))
-    after, before = recv_r[...].astype(F32), recv_l[...].astype(F32)
-    upper = jnp.where(low, after, before)
-    lower = pltpu.roll(jnp.where(low, before, after), RIM, 1)
-    dwell_x[RIM : RIM + 128, COLS:RING] = jnp.where(side_ok, upper, 0.0).astype(BF16)
-    dwell_x[RIM + 128 : RIM + ROWS, COLS:RING] = jnp.where(side_ok, lower, 0.0).astype(BF16)
+    def unpack(begin, after, before, there):
+        after, before = after.astype(F32), before.astype(F32)
+        upper = jnp.where(low, after, before)
+        lower = pltpu.roll(jnp.where(low, before, after), RIM, 1)
+        for half, x in enumerate((upper, lower)):
+            kept = jnp.where(side_ok, x, 0.0)
+            dwell_x[begin + 32 * half : begin + 32 * half + 32, COLS:RING] = jnp.where(there, kept, 0.0).astype(BF16)
+
+    for g in range(4):
+        rows = slice(32 * g, 32 * g + 32)
+        unpack(RIM + 64 * g, recv_r[rows, :], recv_l[rows, :], True)
 
     arrive((0, 1))
     dwell_x[0:RIM, 0:COLS] = rim_up[...]
@@ -324,12 +331,8 @@
 
     arrive((4, 5, 6, 7))
 
-    def corner(before, after, there):
-        x = jnp.where(low, corners[after].astype(F32), corners[before].astype(F32))
-        return jnp.where(there, jnp.where(side_ok, x, 0.0), 0.0).astype(BF16)
-
-    dwell_x[0:RIM, COLS:RING] = corner(0, 1, has_up)
-    dwell_x[RIM + ROWS :, COLS:RING] = corner(2, 3, has_down)
+    unpack(0, corners[1], corners[0], has_up)
+    unpack(RIM + ROWS, corners[3], corners[2], has_down)
 
     for half in range(2):
         product = jnp.dot(
@@ -386,7 +389,7 @@
             pltpu.VMEM((128, COLS), BF16),
             pltpu.VMEM((128, COLS), BF16),
             pltpu.VMEM((128, COLS), BF16),
-            pltpu.VMEM((4, RIM, COLS), BF16),
+            pltpu.VMEM((4, 32, COLS), BF16),
             pltpu.VMEM((ROWS, 3 * COLS), BF16),
             pltpu.VMEM((2, RIM, 3 * COLS), BF16),
             pltpu.VMEM((2, RIM, RING), BF16),

time: 12.9 us -> 12.8 us (level)
  no operation moved by 1% of the time
where the time goes in v6:
time: 12.8 us; the launch traced here: 12.7 us
  Pallas kernels  12 us (94%)
  local copies, waits for them, and re-layouts  0.63 us (5%)
    pallas_call x1, Pallas kernels, tile_step(): pl.pallas_call(functools.partial(kernel, n_space, n_scen), out_shape=pltp...  12 us
    unnamed x1, local copies, waits for them, and re-layouts  0.63 us

profile of v6, /device:TPU:1, one launch (start us, length us, event | category | flops | bytes accessed | tf_op | source)
XLA Modules:
  0.0 12.7 jit_solution(3530349228033792345)
XLA Ops:
  0.0 12.0 %shard_map.82 = bf16[256,128]{1,0:T(8,128)(2,1)S(1)} custom-call(bf16[256,128]{1,0:T(8,128)(2,1)} %dwell_hbm.1, bf16[256,1024]{1,0:T(8,128)(2,1)} %target_hbm.1, s32[2,16]{1,0:T(2,128)} %bitcast.2, s32[1,16]{1,0:T(1,128)} %bitcast.3, f32[4]{0:T(128)} %rate_hbm.1, bf16[4,63]{1,0:T(4,128)(2,1)} %row_hbm.1, bf16[4,63]{1,0:T(4,128)(2,1)} %col_hbm.1, ...), custom_call_target="tpu_custom_call" | custom-call | tf_op jit(solution)/shard_map/pallas_call | solution.py:370
  12.0 0.6 %copy.10 = bf16[256,128]{1,0:T(8,128)(2,1)} copy(bf16[256,128]{1,0:T(8,128)(2,1)S(1)} %shard_map.82) | data formatting | bytes 131072

commit v7 on v6

--- a/solution.py
+++ b/solution.py
@@ -183,6 +183,42 @@
         t_bot[...] = jnp.zeros_like(t_bot)
         rim_down[...] = jnp.zeros_like(rim_down)
 
+    def arrive(ks):
+        for k in ks:
+            pl.when(comes[k])(copies[k].wait_recv)
+
+    side_ok = jnp.where(lanes((1, COLS)) < RIM, jnp.where(has_right, 1, 0), jnp.where(has_left, 1, 0)) > 0
+    low = lanes((1, COLS)) < RIM
+
+    for load in small:
+        load.wait()
+
+    taps8[...] = jnp.zeros_like(taps8)
+    taps8[0:NRATE, 0:TAPS] = row_taps[...].astype(F32)
+    taps8[4 : 4 + NRATE, 0:TAPS] = col_taps[...].astype(F32)
+    taps = taps8[...]
+    flip = jnp.where(
+        lax.broadcasted_iota(jnp.int32, (RING, RING), 0) + lanes((RING, RING)) == TAPS - 1, 1.0, 0.0
+    ).astype(BF16)
+    reversed_taps = jnp.dot(taps.astype(BF16), flip, preferred_element_type=F32)
+
+    def toeplitz(line, count_, first):
+        return pltpu.roll(
+            jnp.broadcast_to(line, (count_, RING)), first % RING, 1, stride=1, stride_axis=0
+        )
+
+    for q in range(NRATE):
+        band = toeplitz(taps[q : q + 1], 192, 1).astype(BF16)
+        row_fwd[0, 160 * q : 160 * q + 160, :] = band[0:160]
+        row_fwd[1, 160 * q : 160 * q + 160, :] = band[32:192]
+        band = toeplitz(taps[4 + q : 5 + q], 320, -RADIUS - 32)
+        col_tall[q] = band[:, 0:COLS]
+        col_mat[q] = band[32 : 32 + RING].astype(BF16)
+        band = toeplitz(reversed_taps[q : q + 1], 192, 1)
+        row_tall[q, 0] = band[:, 0:COLS]
+        row_tall[q, 1] = band[:, COLS:RING]
+        row_adj[:, RING * q : RING * q + RING] = band[0:128].astype(BF16)
+
     pl.semaphore_wait(barrier, greeted)
 
     first_rows, last_rows = slice(0, RIM), slice(ROWS - RIM, ROWS)
@@ -212,42 +248,6 @@
     ]
     for k in (8, 9, 4, 5, 6, 7, 2, 3, 0, 1):
         pl.when(peers[k][2])(copies[k].start)
-
-    def arrive(ks):
-        for k in ks:
-            pl.when(comes[k])(copies[k].wait_recv)
-
-    side_ok = jnp.where(lanes((1, COLS)) < RIM, jnp.where(has_right, 1, 0), jnp.where(has_left, 1, 0)) > 0
-    low = lanes((1, COLS)) < RIM
-
-    for load in small:
-        load.wait()
-
-    taps8[...] = jnp.zeros_like(taps8)
-    taps8[0:NRATE, 0:TAPS] = row_taps[...].astype(F32)
-    taps8[4 : 4 + NRATE, 0:TAPS] = col_taps[...].astype(F32)
-    taps = taps8[...]
-    flip = jnp.where(
-        lax.broadcasted_iota(jnp.int32, (RING, RING), 0) + lanes((RING, RING)) == TAPS - 1, 1.0, 0.0
-    ).astype(BF16)
-    reversed_taps = jnp.dot(taps.astype(BF16), flip, preferred_element_type=F32)
-
-    def toeplitz(line, count_, first):
-        return pltpu.roll(
-            jnp.broadcast_to(line, (count_, RING)), first % RING, 1, stride=1, stride_axis=0
-        )
-
-    for q in range(NRATE):
-        band = toeplitz(taps[q : q + 1], 192, 1).astype(BF16)
-        row_fwd[0, 160 * q : 160 * q + 160, :] = band[0:160]
-        row_fwd[1, 160 * q : 160 * q + 160, :] = band[32:192]
-        band = toeplitz(taps[4 + q : 5 + q], 320, -RADIUS - 32)
-        col_tall[q] = band[:, 0:COLS]
-        col_mat[q] = band[32 : 32 + RING].astype(BF16)
-        band = toeplitz(reversed_taps[q : q + 1], 192, 1)
-        row_tall[q, 0] = band[:, 0:COLS]
-        row_tall[q, 1] = band[:, COLS:RING]
-        row_adj[:, RING * q : RING * q + RING] = band[0:128].astype(BF16)
 
     offs = off_v[...]
     row_at = sp * ROWS + lax.broadcasted_iota(jnp.int32, (OUT, SCEN), 0) - 32 + offs[0:1, :]
@@ -300,6 +300,10 @@
             rim_band[pair, 64:128, lanes_] = jnp.where(low, 0.0, second[64:128]).astype(BF16)
 
     dwell_x[RIM : RIM + ROWS, 0:COLS] = tile[...]
+    for q in range(NRATE):
+        back[RING * q + 192 : RING * q + 256, COLS:RING] = jnp.zeros((64, COLS), BF16)
+    for k in range(10):
+        pl.when(peers[k][2])(copies[k].wait_send)
     arrive((8, 9))
     rims = jnp.concatenate([t_top[...], t_bot[...]], axis=0)
     total = jnp.zeros((128, COLS), F32)
@@ -349,7 +353,6 @@
         product = jnp.dot(misfit, col_mat[q, :, 0:COLS], preferred_element_type=F32).astype(BF16)
         back[RING * q : RING * q + 256, 0:COLS] = product[0:256]
         back[RING * q : RING * q + 192, COLS:RING] = product[128:OUT]
-        back[RING * q + 192 : RING * q + 256, COLS:RING] = jnp.zeros((64, COLS), BF16)
 
     grad = jnp.dot(row_adj[...], back[...], preferred_element_type=F32) - t_grad[...]
     load_bound.wait()
@@ -359,8 +362,6 @@
         stepped = dwell - STEP_SIZE * grad[:, COLS * half : COLS * half + COLS]
         kept = jnp.where(bound_v[rows, :] == 1, jnp.maximum(stepped, 0.0), stepped)
         next_ref[rows, :] = kept.astype(BF16)
-    for k in range(10):
-        pl.when(peers[k][2])(copies[k].wait_send)
 
 
 def tile_step(n_space, n_scen, dwell, target, bound, offsets, level, rates, row_kernels, col_kernels):

time: 12.8 us -> 12.8 us (level)
  no operation moved by 1% of the time
where the time goes in v7:
time: 12.8 us; the launch traced here: 12.7 us
  Pallas kernels  12 us (94%)
  local copies, waits for them, and re-layouts  0.63 us (5%)
    pallas_call x1, Pallas kernels, tile_step(): pl.pallas_call(functools.partial(kernel, n_space, n_scen), out_shape=pltp...  12 us
    unnamed x1, local copies, waits for them, and re-layouts  0.63 us

profile of v7, /device:TPU:1, one launch (start us, length us, event | category | flops | bytes accessed | tf_op | source)
XLA Modules:
  0.0 12.7 jit_solution(4573284677797159868)
XLA Ops:
  0.0 12.0 %shard_map.82 = bf16[256,128]{1,0:T(8,128)(2,1)S(1)} custom-call(bf16[256,128]{1,0:T(8,128)(2,1)} %dwell_hbm.1, bf16[256,1024]{1,0:T(8,128)(2,1)} %target_hbm.1, s32[2,16]{1,0:T(2,128)} %bitcast.2, s32[1,16]{1,0:T(1,128)} %bitcast.3, f32[4]{0:T(128)} %rate_hbm.1, bf16[4,63]{1,0:T(4,128)(2,1)} %row_hbm.1, bf16[4,63]{1,0:T(4,128)(2,1)} %col_hbm.1, ...), custom_call_target="tpu_custom_call" | custom-call | tf_op jit(solution)/shard_map/pallas_call | solution.py:371
  12.0 0.6 %copy.10 = bf16[256,128]{1,0:T(8,128)(2,1)} copy(bf16[256,128]{1,0:T(8,128)(2,1)S(1)} %shard_map.82) | data formatting | bytes 131072

commit v8 on v7

--- a/solution.py
+++ b/solution.py
@@ -177,17 +177,30 @@
     def _():
         t_top[...] = jnp.zeros_like(t_top)
         rim_up[...] = jnp.zeros_like(rim_up)
+        corners[0:2] = jnp.zeros((2, 32, COLS), BF16)
 
     @pl.when(sp == n_space - 1)
     def _():
         t_bot[...] = jnp.zeros_like(t_bot)
         rim_down[...] = jnp.zeros_like(rim_down)
+        corners[2:4] = jnp.zeros((2, 32, COLS), BF16)
+
+    @pl.when(sc == 0)
+    def _():
+        recv_l[...] = jnp.zeros_like(recv_l)
+        for k in (0, 2):
+            corners[k] = jnp.zeros((32, COLS), BF16)
+
+    @pl.when(sc == n_scen - 1)
+    def _():
+        recv_r[...] = jnp.zeros_like(recv_r)
+        for k in (1, 3):
+            corners[k] = jnp.zeros((32, COLS), BF16)
 
     def arrive(ks):
         for k in ks:
             pl.when(comes[k])(copies[k].wait_recv)
 
-    side_ok = jnp.where(lanes((1, COLS)) < RIM, jnp.where(has_right, 1, 0), jnp.where(has_left, 1, 0)) > 0
     low = lanes((1, COLS)) < RIM
 
     for load in small:
@@ -317,17 +330,16 @@
     t_grad[64:128, COLS:RING] += total[64:128]
 
     arrive((2, 3))
-    def unpack(begin, after, before, there):
+    def unpack(begin, after, before):
         after, before = after.astype(F32), before.astype(F32)
         upper = jnp.where(low, after, before)
         lower = pltpu.roll(jnp.where(low, before, after), RIM, 1)
         for half, x in enumerate((upper, lower)):
-            kept = jnp.where(side_ok, x, 0.0)
-            dwell_x[begin + 32 * half : begin + 32 * half + 32, COLS:RING] = jnp.where(there, kept, 0.0).astype(BF16)
+            dwell_x[begin + 32 * half : begin + 32 * half + 32, COLS:RING] = x.astype(BF16)
 
     for g in range(4):
         rows = slice(32 * g, 32 * g + 32)
-        unpack(RIM + 64 * g, recv_r[rows, :], recv_l[rows, :], True)
+        unpack(RIM + 64 * g, recv_r[rows, :], recv_l[rows, :])
 
     arrive((0, 1))
     dwell_x[0:RIM, 0:COLS] = rim_up[...]
@@ -335,8 +347,8 @@
 
     arrive((4, 5, 6, 7))
 
-    unpack(0, corners[1], corners[0], has_up)
-    unpack(RIM + ROWS, corners[3], corners[2], has_down)
+    unpack(0, corners[1], corners[0])
+    unpack(RIM + ROWS, corners[3], corners[2])
 
     for half in range(2):
         product = jnp.dot(

time: 12.8 us -> 12.8 us (level)
  no operation moved by 1% of the time
where the time goes in v8:
time: 12.8 us; the launch traced here: 12.7 us
  Pallas kernels  12 us (94%)
  local copies, waits for them, and re-layouts  0.63 us (5%)
    pallas_call x1, Pallas kernels, tile_step(): pl.pallas_call(functools.partial(kernel, n_space, n_scen), out_shape=pltp...  12 us
    unnamed x1, local copies, waits for them, and re-layouts  0.63 us

profile of v8, /device:TPU:1, one launch (start us, length us, event | category | flops | bytes accessed | tf_op | source)
XLA Modules:
  0.0 12.7 jit_solution(11945471193732412304)
XLA Ops:
  0.0 12.0 %shard_map.82 = bf16[256,128]{1,0:T(8,128)(2,1)S(1)} custom-call(bf16[256,128]{1,0:T(8,128)(2,1)} %dwell_hbm.1, bf16[256,1024]{1,0:T(8,128)(2,1)} %target_hbm.1, s32[2,16]{1,0:T(2,128)} %bitcast.2, s32[1,16]{1,0:T(1,128)} %bitcast.3, f32[4]{0:T(128)} %rate_hbm.1, bf16[4,63]{1,0:T(4,128)(2,1)} %row_hbm.1, bf16[4,63]{1,0:T(4,128)(2,1)} %col_hbm.1, ...), custom_call_target="tpu_custom_call" | custom-call | tf_op jit(solution)/shard_map/pallas_call | solution.py:383
  12.0 0.6 %copy.10 = bf16[256,128]{1,0:T(8,128)(2,1)} copy(bf16[256,128]{1,0:T(8,128)(2,1)S(1)} %shard_map.82) | data formatting | bytes 131072
